TPU v7x, 32 devices: a whole 2x2x4 slice. The times are simulated.
32 devices in a mesh: row: 4 (over y, x), col: 8 (over z, core).
Axes of the slice: x: 2, y: 2, z: 4, core: 2. Of those that a mesh axis runs over, the one named last changes fastest.
Arguments:
- tokens: bfloat16 [1024, 53248], P(('row', 'col')), may hold values from -6 to 6
- eigvecs: float32 [53248, 2048], P('row', 'col'), may hold values from -0.02734375 to 0.02734375
- eigvals: float32 [2048], P('col'), may hold values from 0.25 to 4
- v_first: float32 [53248, 256], P(('row', 'col')), may hold values from -0.109375 to 0.109375
- v_second: float32 [53248, 256], P(('row', 'col')), may hold values from -0.109375 to 0.109375
- t_first: float32 [256, 256], replicated, may hold values from -0.375 to 0.375
- t_second: float32 [256, 256], replicated, may hold values from -0.375 to 0.375
Outputs:
- whitened: float32 [1024, 2048], P('row', 'col')
All inputs are finite; a program needn't handle non-finite values.
Results may differ from a plain program's by a relative error of at most 0.0029.
Values may be sent and summed in bfloat16 or wider, within the bound.
No kernel may reach another device: no remote copies, remote signals or barrier semaphores. Data moves between devices by JAX's collectives and lax.ppermute only.
A program may use at most 128 MiB of HBM per device.

v0:
```python
import jax
import jax.numpy as jnp
from jax import lax
from jax.sharding import PartitionSpec as P


def local_update(block, panel, factor, inner):
    middle = jnp.dot(
        factor, inner, precision=lax.Precision.HIGHEST, preferred_element_type=jnp.float32
    )
    return block - jnp.dot(
        panel, middle, precision=lax.Precision.HIGHEST, preferred_element_type=jnp.float32
    )


def partial_inner(panel, block):
    return jnp.dot(
        panel.T, block, precision=lax.Precision.HIGHEST, preferred_element_type=jnp.float32
    )


def per_device(tokens, eigvecs, eigvals, v_first, v_second, t_first, t_second):
    block = lax.all_to_all(eigvecs, "col", split_axis=0, concat_axis=1, tiled=True)
    for panel, factor in ((v_second, t_second), (v_first, t_first)):
        inner = lax.psum(partial_inner(panel, block), ("row", "col"))
        block = local_update(block, panel, factor, inner)
    every_value = lax.all_gather(eigvals, "col", axis=0, tiled=True)
    whitening = (block * lax.rsqrt(every_value)[None, :]).astype(jnp.bfloat16)
    slab = lax.all_to_all(tokens, ("row", "col"), split_axis=1, concat_axis=0, tiled=True)
    partial_value = jnp.dot(slab, whitening, preferred_element_type=jnp.float32)
    by_column = lax.psum_scatter(partial_value, "col", scatter_dimension=1, tiled=True)
    summed = lax.psum_scatter(by_column, "row", scatter_dimension=0, tiled=True)
    return summed


def solution(mesh):
    in_specs = (
        P(("row", "col"), None),
        P("row", "col"),
        P("col"),
        P(("row", "col"), None),
        P(("row", "col"), None),
        P(),
        P(),
    )
    out_specs = P("row", "col")
    return jax.shard_map(
        per_device, mesh=mesh, in_specs=in_specs, out_specs=out_specs, check_vma=False
    )
```

profile of v0, /device:TPU:0, one launch (start us, length us, event | category | flops | bytes accessed | tf_op | source)
XLA Modules:
  0.0 837.7 jit_solution(9575933095389601247)
XLA Ops:
  6.5 0.0 copy-start
  6.5 13.8 %copy.15 = f32[8,1664,256]{1,2,0:T(8,128)} copy(f32[8,1664,256]{2,1,0:T(8,128)} %bitcast.39) | data formatting | bytes 27262976 | tf_op jit(solution)/shard_map/all_to_all | solution.py:23
  20.4 6.4 all-to-all-start
  26.7 4.1 copy.20
  30.8 292.2 %all-to-all-done = f32[8,1664,256]{1,2,0:T(8,128)} async-done(((f32[8,1664,256]{1,2,0:T(8,128)}), f32[8,1664,256]{1,2,0:T(8,128)}, u32[]{:S(2)}, u32[]{:S(2)}) %all-to-all-start) | async-done | bytes 13631520 | tf_op jit(solution)/shard_map/all_to_all | solution.py:23
  323.0 4.1 all-to-all-start.1
  327.2 0.0 all-reduce.3.cloned.1.call-start
  327.2 25.8 %fusion.2 = f32[256,2048]{1,0:T(8,128)} fusion(f32[1664,256]{1,0:T(8,128)S(1)} %copy-done, f32[1664,2048]{0,1:T(8,128)} %bitcast.2), kind=kOutput, calls=%fused_computation.7 | convolution fusion | flops 10468982784 | bytes 17432576 | tf_op jit(solution)/shard_map/dot_general | solution.py:17
  353.1 0.0 all-reduce.3.cloned.1.call-update
  353.1 0.2 all-reduce.5.cloned.1.call-start
  353.3 151.8 %all-reduce.3.cloned.1.call-done = f32[256,2048]{1,0:T(8,128)} async-done(((f32[256,2048]{1,0:T(8,128)}), f32[256,2048]{1,0:T(8,128)}) %all-reduce.3.cloned.1.call-update) | async-done | bytes 2097168 | tf_op jit(solution)/shard_map/psum | solution.py:25
  505.2 5.2 fusion.3
  510.3 0.0 copy-start.3
  510.3 16.9 %bitcast_subtract_fusion.1 = f32[1664,2048]{0,1:T(8,128)S(1)} fusion(f32[1664,2048]{0,1:T(8,128)} %bitcast.2, f32[2048,256]{1,0:T(8,128)S(1)} %fusion.3, f32[1664,256]{1,0:T(8,128)S(1)} %copy-done), kind=kOutput, calls=%fused_computation.3 | convolution fusion | flops 10472390656 | bytes 31064064 | tf_op jit(solution)/shard_map/dot_general | solution.py:11
  527.3 4.9 copy-done.2
  532.1 13.1 %convolution_bitcast_fusion.1 = f32[256,2048]{0,1:T(8,128)} fusion(f32[1664,2048]{0,1:T(8,128)S(1)} %bitcast_subtract_fusion.1, f32[1664,256]{1,0:T(8,128)S(1)} %copy-done.3), kind=kOutput, calls=%fused_computation.6 | convolution fusion | flops 10468982784 | bytes 17432576 | tf_op jit(solution)/shard_map/dot_general | solution.py:17
  545.3 0.0 all-reduce.5.cloned.1.call-update
  545.3 0.0 reduce-scatter.3.cloned.1.call-start
  545.4 0.6 copy-done.6
  546.0 10.6 %all-gather = f32[8,1,256]{2,1,0:T(1,128)S(1)} all-gather(f32[1,1,256]{2,1,0:T(1,128)S(1)} %bitcast.43), channel_id=1, replica_groups=mesh['row'=4,'col'=8] {'col'}, dimensions={0}, use_global_device_ids=true | all-gather | bytes 9216 | tf_op jit(solution)/shard_map/all_gather | solution.py:27
  556.6 122.3 %all-reduce.5.cloned.1.call-done = f32[256,2048]{0,1:T(8,128)} async-done(((f32[256,2048]{0,1:T(8,128)}), f32[256,2048]{0,1:T(8,128)}) %all-reduce.5.cloned.1.call-update) | async-done | bytes 2097168 | tf_op jit(solution)/shard_map/psum | solution.py:25
  678.9 3.5 fusion.4
  682.4 16.4 %fusion.1 = bf16[1664,2048]{0,1:T(8,128)(2,1)} fusion(f32[1664,2048]{0,1:T(8,128)} %copy-done.2, f32[2048,256]{1,0:T(8,128)S(1)} %fusion.4, f32[1664,256]{1,0:T(8,128)S(1)} %copy-done.3, f32[2048]{0:T(1024)S(1)} %bitcast.42), kind=kOutput, calls=%fused_computation.2 | convolution fusion | flops 10479206400 | bytes 24256512 | tf_op jit(solution)/shard_map/dot_general | solution.py:11
  698.8 0.0 all-to-all-done.1
  698.8 12.9 %convolution_bitcast_fusion = f32[1024,2048]{0,1:T(8,128)} fusion(bf16[1664,2048]{0,1:T(8,128)(2,1)} %fusion.1, bf16[1024,1664]{1,0:T(8,128)(2,1)} %bitcast.10), kind=kOutput, calls=%fused_computation.4 | convolution fusion | flops 6979321856 | bytes 18612224 | tf_op jit(solution)/shard_map/dot_general | solution.py:30
  711.8 0.0 reduce-scatter.3.cloned.1.call-update
  711.8 0.0 copy-start.1
  711.8 0.0 reduce-scatter.5.cloned.1.call-start
  711.9 88.4 %reduce-scatter.3.cloned.1.call-done = f32[1024,256]{0,1:T(8,128)} async-done(((f32[1024,2048]{0,1:T(8,128)}), f32[1024,256]{0,1:T(8,128)}) %reduce-scatter.3.cloned.1.call-update) | async-done | bytes 1048592 | tf_op jit(solution)/shard_map/reduce_scatter | solution.py:31
  800.2 0.0 reduce-scatter.5.cloned.1.call-update
  800.2 29.2 %reduce-scatter.5.cloned.1.call-done = f32[256,256]{0,1:T(8,128)} async-done(((f32[1024,256]{0,1:T(8,128)}), f32[256,256]{0,1:T(8,128)}) %reduce-scatter.5.cloned.1.call-update) | async-done | bytes 262160 | tf_op jit(solution)/shard_map/reduce_scatter | solution.py:32
  829.4 1.8 copy.17
  (10 shorter events, 0.0 us)
Async XLA Ops:
  6.5 320.7 %copy-start = (f32[1664,256]{1,0:T(8,128)S(1)}, f32[1664,256]{1,0:T(8,128)}, u32[]{:S(2)}) copy-start(f32[1664,256]{1,0:T(8,128)} %param.11) | copy-start | bytes 5111812
  20.4 302.7 %all-to-all-start = ((f32[8,1664,256]{1,2,0:T(8,128)}), f32[8,1664,256]{1,2,0:T(8,128)}, u32[]{:S(2)}, u32[]{:S(2)}) async-start(f32[8,1664,256]{1,2,0:T(8,128)} %copy.15), calls=%async_computation | async-start | bytes 27262976 | tf_op jit(solution)/shard_map/all_to_all | solution.py:23
  323.0 375.8 %all-to-all-start.1 = ((bf16[32,32,1664]{2,0,1:T(8,128)(2,1)}), bf16[32,32,1664]{2,0,1:T(8,128)(2,1)}, u32[]{:S(2)}, u32[]{:S(2)}) async-start(bf16[32,32,1664]{2,0,1:T(8,128)(2,1)} %bitcast.40), calls=%async_computation.1 | async-start | bytes 6815744 | tf_op jit(solution)/shard_map/all_to_all | solution.py:29
  327.2 178.0 %all-reduce.3.cloned.1.call-start = ((), (), s32[]{:S(2)}) async-start(), calls=%async_computation.4 | async-start | bytes 4194304 | tf_op jit(solution)/shard_map/psum | solution.py:25
  353.1 152.1 %copy-start.4 = (f32[256,256]{1,0:T(8,128)S(1)}, f32[256,256]{1,0:T(8,128)}, u32[]{:S(2)}) copy-start(f32[256,256]{1,0:T(8,128)} %param.13) | copy-start | bytes 786436
  353.1 325.8 %all-reduce.5.cloned.1.call-start = ((), (), s32[]{:S(2)}) async-start(), calls=%async_computation.5 | async-start | bytes 4194304 | tf_op jit(solution)/shard_map/psum | solution.py:25
  510.3 21.8 %copy-start.3 = (f32[1664,256]{1,0:T(8,128)S(1)}, f32[1664,256]{1,0:T(8,128)}, u32[]{:S(2)}) copy-start(f32[1664,256]{1,0:T(8,128)} %param.10) | copy-start | bytes 5111812
  527.2 4.9 copy-start.2
  545.3 0.7 copy-start.6
  545.3 133.6 %copy-start.5 = (f32[256,256]{1,0:T(8,128)S(1)}, f32[256,256]{1,0:T(8,128)}, u32[]{:S(2)}) copy-start(f32[256,256]{1,0:T(8,128)} %param.12) | copy-start | bytes 786436
  545.3 254.9 %reduce-scatter.3.cloned.1.call-start = ((), (), s32[]{:S(2)}) async-start(), calls=%async_computation.6 | async-start | bytes 9437184 | tf_op jit(solution)/shard_map/reduce_scatter | solution.py:31
  711.8 119.4 %copy-start.1 = (f32[1664,256]{1,0:T(8,128)S(1)}, f32[1664,256]{1,0:T(8,128)}, u32[]{:S(2)}) copy-start(f32[1664,256]{1,0:T(8,128)} %param.11) | copy-start | bytes 5111812
  711.8 117.6 %reduce-scatter.5.cloned.1.call-start = ((), (), s32[]{:S(2)}) async-start(), calls=%async_computation.7 | async-start | bytes 1310720 | tf_op jit(solution)/shard_map/reduce_scatter | solution.py:32
Sparse Core Ops, SparseCore 0:
  353.2 151.8 all-reduce.2
  545.4 133.4 all-reduce.4
  711.9 88.2 reduce-scatter.2
  803.0 26.4 reduce-scatter.4
where the time goes:
time: 838 us
  waiting for transfers between devices  684 us (82%)
  matrix products  93.9 us (11%)
  local copies, waits for them, and re-layouts  25.3 us (3%)
  between operations  13.2 us (2%)
  starting transfers between devices  10.8 us (1%)
  blocking collectives  10.6 us (1%)
    all_to_all x1, waiting for transfers between devices, per_device(): lax.all_to_all(eigvecs, 'col', split_axis=0, concat_axis=1, tiled=True)  292 us
    psum x2, waiting for transfers between devices, per_device(): inner = lax.psum(partial_inner(panel, block), ('row', 'col'))  274 us
    reduce_scatter x1, waiting for transfers between devices, per_device(): lax.psum_scatter(partial_value, 'col', scatter_dimension=1, tiled=True)  88.4 us
    dot_general x2, matrix products, partial_inner(): jnp.dot(panel.T, block, precision=lax.Precision.HIGHEST, preferred_elemen...  39 us
    dot_general x2, matrix products, local_update(): jnp.dot(panel, middle, precision=lax.Precision.HIGHEST, preferred_element...  33.3 us
    reduce_scatter x1, waiting for transfers between devices, per_device(): summed = lax.psum_scatter(by_column, 'row', scatter_dimension=0, tiled=True)  29.2 us
  transfers between devices with their start and end apart: 6, of which 5 were waited for; matrix products, arithmetic and copies ran while one was open for 10% of the time, Pallas kernels for 0%

commit v1 on v0

v1 whole, which is shorter than its diff:
```python
import jax
import jax.numpy as jnp
from jax import lax
from jax.sharding import PartitionSpec as P

HIGHEST = lax.Precision.HIGHEST
CHUNKS = 2


def dot32(a, b):
    return jnp.dot(a, b, precision=HIGHEST, preferred_element_type=jnp.float32)


def dot16(a, b):
    return jnp.dot(a, b, preferred_element_type=jnp.float32)


def split(v):
    high = lax.reduce_precision(v, 8, 7)
    return high.astype(jnp.bfloat16), (v - high).astype(jnp.bfloat16)


def make(rows, cols):
    swap = [(i, i ^ 1) for i in range(cols)]
    groups = [[i for i in range(cols) if i % 2 == core] for core in range(2)]
    half = cols // 2

    def row_sum(x):
        return jnp.sum(lax.all_to_all(x, "row", split_axis=0, concat_axis=0, tiled=True), axis=0)

    def core_sum(parts, core):
        even = jnp.stack(parts[0::2])
        odd = jnp.stack(parts[1::2])
        mine = jnp.where(core == 0, even, odd)
        other = jnp.where(core == 0, odd, even)
        return mine + lax.ppermute(other, "col", swap)

    def z_sum(x):
        got = lax.all_to_all(x, "col", split_axis=0, concat_axis=0, tiled=True, axis_index_groups=groups)
        return jnp.sum(got, axis=0)

    def per_device(tokens, eigvecs, eigvals, v_first, v_second, t_first, t_second):
        nb = v_first.shape[1]
        core = lax.axis_index("col") % 2
        slab = lax.all_to_all(tokens, ("row", "col"), split_axis=1, concat_axis=0, tiled=True)
        tok = slab.shape[0]
        depth, width = v_first.shape[0], eigvecs.shape[1]
        high, low = split(jnp.concatenate([v_first, v_second], axis=1))
        along = dot16(slab, high) + dot16(slab, low)
        gram = dot32(v_first.T, v_second)
        packed = jnp.concatenate([
            along.reshape(rows, tok // rows, 2 * nb),
            jnp.broadcast_to(gram.reshape(1, nb // 2, 2 * nb), (rows, nb // 2, 2 * nb)),
        ], axis=1)
        packed = packed.reshape(rows * packed.shape[1], 2 * nb)
        packed = lax.psum(lax.psum_scatter(packed, "row", scatter_dimension=0, tiled=True), "col")
        along = packed[: tok // rows]
        gram = packed[tok // rows:].reshape(nb, nb)

        outs = []
        step = width // CHUNKS
        for j in range(CHUNKS):
            piece = eigvecs[:, j * step:(j + 1) * step].astype(jnp.bfloat16).reshape(cols, depth, step)
            piece = lax.all_to_all(piece, "col", split_axis=0, concat_axis=0, tiled=True)
            parts = []
            for s in range(cols):
                w = piece[s]
                p = dot16(slab, w)
                i = dot16(high.T, w) + dot16(low.T, w)
                parts.append(jnp.concatenate([p.reshape(rows, tok // rows, step), i.reshape(rows, 2 * nb // rows, step)], axis=1))
            summed = core_sum(parts, core)
            summed = row_sum(jnp.swapaxes(summed, 0, 1))
            summed = z_sum(summed)
            base = summed[: tok // rows]
            inner = summed[tok // rows:]
            inner = lax.all_to_all(jnp.broadcast_to(inner[None], (rows, *inner.shape)), "row", split_axis=0, concat_axis=0, tiled=True)
            inner = inner.reshape(2 * nb, step)
            m_second = dot32(t_second, inner[nb:])
            m_first = dot32(t_first, inner[:nb] - dot32(gram, m_second))
            scale = lax.rsqrt(eigvals[j * step:(j + 1) * step])
            outs.append((base - dot32(along[:, nb:], m_second) - dot32(along[:, :nb], m_first)) * scale[None, :])
        return jnp.concatenate(outs, axis=1)

    return per_device


def solution(mesh):
    in_specs = (
        P(("row", "col"), None),
        P("row", "col"),
        P("col"),
        P(("row", "col"), None),
        P(("row", "col"), None),
        P(),
        P(),
    )
    out_specs = P("row", "col")
    body = make(mesh.shape["row"], mesh.shape["col"])
    return jax.shard_map(body, mesh=mesh, in_specs=in_specs, out_specs=out_specs, check_vma=False)
```

time: 838 us -> 564 us (0.67)
  waiting for transfers between devices: 684 us -> 248 us
  blocking collectives: 10.6 us -> 83.4 us
  matrix products: 93.9 us -> 122 us
  other arithmetic: 0 us -> 24.4 us
  starting transfers between devices: 10.8 us -> 32.4 us
    psum x2 -> x1, waiting for transfers between devices: 274 us -> 36.4 us  [per_device(): lax.psum(lax.psum_scatter(packed, 'row', scatter_dimension=0, tiled=True)...]
    reduce_scatter x2 -> x1, waiting for transfers between devices: 118 us -> 0.02 us  [per_device(): lax.psum_scatter(packed, 'row', scatter_dimension=0, tiled=True)]
    all_to_all x1 -> x7, waiting for transfers between devices: 292 us -> 178 us  [the longest x2 71.1 us: row_sum(): lax.all_to_all(x, 'row', split_axis=0, concat_axis=0, tiled=True)]
    all_to_all x0 -> x1, blocking collectives: none -> 83.4 us  [per_device(): lax.all_to_all(piece, 'col', split_axis=0, concat_axis=0, tiled=True)]
    all_to_all x1, waiting for transfers between devices: 0.01 us -> 33.6 us  [per_device(): lax.all_to_all(tokens, ('row', 'col'), split_axis=1, concat_axis=0, tiled...]
    dot_general x7 -> x61, matrix products: 93.9 us -> 122 us  [the longest x50 114 us: dot16(): return jnp.dot(a, b, preferred_element_type=jnp.float32)]
    all_to_all x1 -> x7, starting transfers between devices: 6.35 us -> 27.6 us  [the longest x2 8.41 us: row_sum(): lax.all_to_all(x, 'row', split_axis=0, concat_axis=0, tiled=True)]
    all_to_all x1 -> x0, local copies, waits for them, and re-layouts: 13.8 us -> none  [per_device(): lax.all_to_all(eigvecs, 'col', split_axis=0, concat_axis=1, tiled=True)]
  transfers between devices with their start and end apart: 6 -> 12, of which waited for: 5 -> 8; matrix products, arithmetic and copies ran while one was open for 10% -> 23% of each run, Pallas kernels for 0% -> 0%
where the time goes in v1:
time: 564 us; the launch traced here: 557 us
  waiting for transfers between devices  248 us (44%)
  matrix products  122 us (22%)
  blocking collectives  83.4 us (15%)
  starting transfers between devices  32.4 us (6%)
  local copies, waits for them, and re-layouts  31 us (5%)
  other arithmetic  24.4 us (4%)
  between operations  15.1 us (3%)
    dot_general x50, matrix products, dot16(): return jnp.dot(a, b, preferred_element_type=jnp.float32)  114 us
    all_to_all x1, blocking collectives, per_device(): lax.all_to_all(piece, 'col', split_axis=0, concat_axis=0, tiled=True)  83.4 us
    all_to_all x2, waiting for transfers between devices, row_sum(): lax.all_to_all(x, 'row', split_axis=0, concat_axis=0, tiled=True)  71.1 us
    all_to_all x1, waiting for transfers between devices, per_device(): lax.all_to_all(piece, 'col', split_axis=0, concat_axis=0, tiled=True)  62 us
    all_to_all x2, waiting for transfers between devices, z_sum(): lax.all_to_all(x, 'col', split_axis=0, concat_axis=0, tiled=True, axis_in...  39.7 us
    psum x1, waiting for transfers between devices, per_device(): lax.psum(lax.psum_scatter(packed, 'row', scatter_dimension=0, tiled=True)...  36.4 us
    all_to_all x1, waiting for transfers between devices, per_device(): lax.all_to_all(tokens, ('row', 'col'), split_axis=1, concat_axis=0, tiled...  33.6 us
  transfers between devices with their start and end apart: 12, of which 8 were waited for; matrix products, arithmetic and copies ran while one was open for 23% of the time, Pallas kernels for 0%

profile of v1, /device:TPU:0, one launch (start us, length us, event | category | flops | bytes accessed | tf_op | source)
XLA Modules:
  0.0 556.8 jit_solution(4502269078186748890)
XLA Ops:
  6.5 5.5 convert.4
  14.0 83.4 %all_to_all.59 = bf16[8,1664,128]{2,1,0:T(8,128)(2,1)} all-to-all(bf16[8,1664,128]{2,1,0:T(8,128)(2,1)S(1)} %bitcast.272), channel_id=1, replica_groups=mesh['row'=4,'col'=8] {'col'}, dimensions={0} | all-to-all | bytes 6815744 | tf_op jit(solution)/shard_map/all_to_all | solution.py:64
  97.3 4.5 all-to-all-start.5
  101.8 4.2 copy.39
  116.9 62.0 %all-to-all-done.5 = bf16[8,1664,128]{2,1,0:T(8,128)(2,1)} async-done(((bf16[8,1664,128]{2,1,0:T(8,128)(2,1)}), bf16[8,1664,128]{2,1,0:T(8,128)(2,1)}, u32[]{:S(2)}, u32[]{:S(2)}) %all-to-all-start.5) | async-done | bytes 3407904 | tf_op jit(solution)/shard_map/all_to_all | solution.py:64
  179.0 4.1 all-to-all-start
  227.1 33.6 %all-to-all-done = bf16[32,32,1664]{2,0,1:T(8,128)(2,1)} async-done(((bf16[32,32,1664]{2,0,1:T(8,128)(2,1)}), bf16[32,32,1664]{2,0,1:T(8,128)(2,1)}, u32[]{:S(2)}, u32[]{:S(2)}) %all-to-all-start) | async-done | bytes 3407904 | tf_op jit(solution)/shard_map/all_to_all | solution.py:45
  260.7 3.2 fusion.75
  273.5 3.6 fusion.55
  280.3 3.6 fusion.45
  298.8 3.1 fusion.30
  303.1 3.6 fusion.15
  306.8 3.1 fusion.20
  310.1 3.6 fusion.10
  313.8 3.1 fusion.5
  320.7 3.7 fusion.141
  328.0 6.1 %fusion.140 = f32[512,1024]{1,0:T(8,128)} fusion(bf16[1664,512]{1,0:T(8,128)(2,1)} %copy-done.1, bf16[1024,1664]{1,0:T(8,128)(2,1)} %bitcast.37), kind=kOutput, calls=%fused_computation.194 | convolution fusion | flops 1744830464 | bytes 7208960 | tf_op jit(solution)/shard_map/dot_general | solution.py:15
  338.5 4.7 all-to-all-start.2
  343.2 6.1 %add_bitcast_fusion.2 = f32[1024,512]{0,1:T(8,128)} fusion(f32[512,1024]{1,0:T(8,128)} %fusion.140, bf16[1664,512]{1,0:T(8,128)(2,1)S(1)} %get-tuple-element.7, bf16[1024,1664]{1,0:T(8,128)(2,1)} %bitcast.37), kind=kOutput, calls=%fused_computation.11 | convolution fusion | flops 1745354752 | bytes 9306112 | tf_op jit(solution)/shard_map/dot_general | solution.py:15
  349.3 3.2 reshape.135
  364.8 30.8 %all-to-all-done.2 = f32[4,4,384,128]{3,2,1,0:T(8,128)} async-done(((f32[4,4,384,128]{3,2,1,0:T(8,128)}), f32[4,4,384,128]{3,2,1,0:T(8,128)}, u32[]{:S(2)}, u32[]{:S(2)}) %all-to-all-start.2) | async-done | bytes 3145760 | tf_op jit(solution)/shard_map/all_to_all | solution.py:29
  395.5 3.7 all-to-all-start.6
  399.3 3.2 reduce_sum.36
  402.5 40.4 %all-to-all-done.6 = f32[4,4,384,128]{3,2,1,0:T(8,128)S(1)} async-done(((f32[4,4,384,128]{3,2,1,0:T(8,128)}), f32[4,4,384,128]{3,2,1,0:T(8,128)S(1)}, u32[]{:S(2)}, u32[]{:S(2)}) %all-to-all-start.6) | async-done | bytes 3145760 | tf_op jit(solution)/shard_map/all_to_all | solution.py:29
  442.9 4.2 all-to-all-start.3
  448.2 18.5 %all-to-all-done.3 = f32[4,384,128]{2,1,0:T(8,128)} async-done(((f32[4,384,128]{2,1,0:T(8,128)}), f32[4,384,128]{2,1,0:T(8,128)}, u32[]{:S(2)}, u32[]{:S(2)}) %all-to-all-start.3) | async-done | bytes 786464 | tf_op jit(solution)/shard_map/all_to_all | solution.py:39
  466.7 3.5 all-to-all-start.7
  472.2 21.1 %all-to-all-done.7 = f32[4,384,128]{2,1,0:T(8,128)S(1)} async-done(((f32[4,384,128]{2,1,0:T(8,128)}), f32[4,384,128]{2,1,0:T(8,128)S(1)}, u32[]{:S(2)}, u32[]{:S(2)}) %all-to-all-start.7) | async-done | bytes 786464 | tf_op jit(solution)/shard_map/all_to_all | solution.py:39
  494.1 3.4 all-to-all-start.4
  497.6 36.4 %all-reduce.2.cloned.1.call-done = f32[384,512]{1,0:T(8,128)} async-done(((f32[384,512]{1,0:T(8,128)}), f32[384,512]{1,0:T(8,128)}) %all-reduce.2.cloned.1.call-update) | async-done | bytes 786448 | tf_op jit(solution)/shard_map/psum | solution.py:56
  536.0 3.6 all-to-all-start.8
  540.1 4.9 all-to-all-done.8
  (213 shorter events, 119.8 us)
Async XLA Ops:
  6.5 533.2 %copy-start = (f32[256,256]{1,0:T(8,128)S(1)}, f32[256,256]{1,0:T(8,128)}, u32[]{:S(2)}) copy-start(f32[256,256]{1,0:T(8,128)} %param.13) | copy-start | bytes 786436
  97.3 81.6 %all-to-all-start.5 = ((bf16[8,1664,128]{2,1,0:T(8,128)(2,1)}), bf16[8,1664,128]{2,1,0:T(8,128)(2,1)}, u32[]{:S(2)}, u32[]{:S(2)}) async-start(bf16[8,1664,128]{2,1,0:T(8,128)(2,1)} %bitcast.271), calls=%async_computation.6 | async-start | bytes 6815744 | tf_op jit(solution)/shard_map/all_to_all | solution.py:64
  108.2 8.0 %copy-start.1 = (bf16[1664,512]{1,0:T(8,128)(2,1)}, bf16[1664,512]{1,0:T(8,128)(2,1)S(1)}, u32[]{:S(2)}) copy-start(bf16[1664,512]{1,0:T(8,128)(2,1)S(1)} %get-tuple-element.8) | copy-start | bytes 5111812
  179.0 81.7 %all-to-all-start = ((bf16[32,32,1664]{2,0,1:T(8,128)(2,1)}), bf16[32,32,1664]{2,0,1:T(8,128)(2,1)}, u32[]{:S(2)}, u32[]{:S(2)}) async-start(bf16[32,32,1664]{2,0,1:T(8,128)(2,1)} %bitcast.270), calls=%async_computation | async-start | bytes 6815744 | tf_op jit(solution)/shard_map/all_to_all | solution.py:45
  273.4 13.7 %copy-start.10 = (f32[1,4,384,128]{3,2,1,0:T(8,128)}, f32[1,4,384,128]{3,2,1,0:T(8,128)S(1)}, u32[]{:S(2)}) copy-start(f32[1,4,384,128]{3,2,1,0:T(8,128)S(1)} %get-tuple-element.25) | copy-start | bytes 2359300
  273.4 13.7 %copy-start.12 = (f32[1,4,384,128]{3,2,1,0:T(8,128)}, f32[1,4,384,128]{3,2,1,0:T(8,128)S(1)}, u32[]{:S(2)}) copy-start(f32[1,4,384,128]{3,2,1,0:T(8,128)S(1)} %get-tuple-element.26) | copy-start | bytes 2359300
  280.3 6.9 %copy-start.18 = (f32[1,4,384,128]{3,2,1,0:T(8,128)}, f32[1,4,384,128]{3,2,1,0:T(8,128)S(1)}, u32[]{:S(2)}) copy-start(f32[1,4,384,128]{3,2,1,0:T(8,128)S(1)} %get-tuple-element.27) | copy-start | bytes 2359300
  280.3 6.9 %copy-start.20 = (f32[1,4,384,128]{3,2,1,0:T(8,128)}, f32[1,4,384,128]{3,2,1,0:T(8,128)S(1)}, u32[]{:S(2)}) copy-start(f32[1,4,384,128]{3,2,1,0:T(8,128)S(1)} %get-tuple-element.28) | copy-start | bytes 2359300
  289.4 44.6 %collective-permute-start = (f32[4,4,384,128]{3,2,1,0:T(8,128)}, f32[4,4,384,128]{3,2,1,0:T(8,128)}, u32[]{:S(2)}, u32[]{:S(2)}) collective-permute-start(f32[4,4,384,128]{3,2,1,0:T(8,128)} %fusion.2), channel_id=1, source_target_pairs={{0,1},{1,0},{2,3},{3,2},{4,5},{5,4},{6,7},{7,6},{8,9},{9,8},{10,11... | collective-permute-start | bytes 9437192 | tf_op jit(solution)/shard_map/ppermute | solution.py:36
  302.1 14.9 %copy-start.6 = (f32[1,4,384,128]{3,2,1,0:T(8,128)}, f32[1,4,384,128]{3,2,1,0:T(8,128)S(1)}, u32[]{:S(2)}) copy-start(f32[1,4,384,128]{3,2,1,0:T(8,128)S(1)} %get-tuple-element.15) | copy-start | bytes 2359300
  302.1 14.9 %copy-start.8 = (f32[1,4,384,128]{3,2,1,0:T(8,128)}, f32[1,4,384,128]{3,2,1,0:T(8,128)S(1)}, u32[]{:S(2)}) copy-start(f32[1,4,384,128]{3,2,1,0:T(8,128)S(1)} %get-tuple-element.16) | copy-start | bytes 2359300
  303.1 14.0 %copy-start.14 = (f32[1,4,384,128]{3,2,1,0:T(8,128)}, f32[1,4,384,128]{3,2,1,0:T(8,128)S(1)}, u32[]{:S(2)}) copy-start(f32[1,4,384,128]{3,2,1,0:T(8,128)S(1)} %get-tuple-element.17) | copy-start | bytes 2359300
  303.1 14.0 %copy-start.16 = (f32[1,4,384,128]{3,2,1,0:T(8,128)}, f32[1,4,384,128]{3,2,1,0:T(8,128)S(1)}, u32[]{:S(2)}) copy-start(f32[1,4,384,128]{3,2,1,0:T(8,128)S(1)} %get-tuple-element.18) | copy-start | bytes 2359300
  310.1 7.0 %copy-start.22 = (f32[1,4,384,128]{3,2,1,0:T(8,128)}, f32[1,4,384,128]{3,2,1,0:T(8,128)S(1)}, u32[]{:S(2)}) copy-start(f32[1,4,384,128]{3,2,1,0:T(8,128)S(1)} %get-tuple-element.19) | copy-start | bytes 2359300
  310.1 7.0 %copy-start.23 = (f32[1,4,384,128]{3,2,1,0:T(8,128)}, f32[1,4,384,128]{3,2,1,0:T(8,128)S(1)}, u32[]{:S(2)}) copy-start(f32[1,4,384,128]{3,2,1,0:T(8,128)S(1)} %get-tuple-element.20) | copy-start | bytes 2359300
  319.4 38.6 %collective-permute-start.1 = (f32[4,4,384,128]{3,2,1,0:T(8,128)}, f32[4,4,384,128]{3,2,1,0:T(8,128)}, u32[]{:S(2)}, u32[]{:S(2)}) collective-permute-start(f32[4,4,384,128]{3,2,1,0:T(8,128)} %fusion.1), channel_id=1, source_target_pairs={{0,1},{1,0},{2,3},{3,2},{4,5},{5,4},{6,7},{7,6},{8,9},{9,8},{10,11... | collective-permute-start | bytes 9437192 | tf_op jit(solution)/shard_map/ppermute | solution.py:36
  328.0 6.1 %copy-start.13 = (f32[1,4,384,128]{3,2,1,0:T(8,128)S(1)}, f32[1,4,384,128]{3,2,1,0:T(8,128)}, u32[]{:S(2)}) copy-start(f32[1,4,384,128]{3,2,1,0:T(8,128)} %copy-done.12) | copy-start | bytes 2359300
  328.0 6.1 %copy-start.19 = (f32[1,4,384,128]{3,2,1,0:T(8,128)S(1)}, f32[1,4,384,128]{3,2,1,0:T(8,128)}, u32[]{:S(2)}) copy-start(f32[1,4,384,128]{3,2,1,0:T(8,128)} %copy-done.18) | copy-start | bytes 2359300
  328.0 6.1 %copy-start.21 = (f32[1,4,384,128]{3,2,1,0:T(8,128)S(1)}, f32[1,4,384,128]{3,2,1,0:T(8,128)}, u32[]{:S(2)}) copy-start(f32[1,4,384,128]{3,2,1,0:T(8,128)} %copy-done.20) | copy-start | bytes 2359300
  328.0 6.2 %copy-start.25 = (f32[1,4,384,128]{3,2,1,0:T(8,128)S(1)}, f32[1,4,384,128]{3,2,1,0:T(8,128)}, u32[]{:S(2)}) copy-start(f32[1,4,384,128]{3,2,1,0:T(8,128)} %copy-done.24) | copy-start | bytes 2359300
  328.0 6.2 %copy-start.27 = (f32[1,4,384,128]{3,2,1,0:T(8,128)S(1)}, f32[1,4,384,128]{3,2,1,0:T(8,128)}, u32[]{:S(2)}) copy-start(f32[1,4,384,128]{3,2,1,0:T(8,128)} %copy-done.26) | copy-start | bytes 2359300
  338.5 57.1 %all-to-all-start.2 = ((f32[4,4,384,128]{3,2,1,0:T(8,128)}), f32[4,4,384,128]{3,2,1,0:T(8,128)}, u32[]{:S(2)}, u32[]{:S(2)}) async-start(f32[4,4,384,128]{3,2,1,0:T(8,128)} %copy.28), calls=%async_computation.2 | async-start | bytes 6291456 | tf_op jit(solution)/shard_map/all_to_all | solution.py:29
  343.2 127.2 %reduce-scatter.2.cloned.1.call-start = ((), (), s32[]{:S(2)}) async-start(), calls=%async_computation.10 | async-start | bytes 3932160 | tf_op jit(solution)/shard_map/reduce_scatter | solution.py:56
  395.5 47.3 %all-to-all-start.6 = ((f32[4,4,384,128]{3,2,1,0:T(8,128)}), f32[4,4,384,128]{3,2,1,0:T(8,128)S(1)}, u32[]{:S(2)}, u32[]{:S(2)}) async-start(f32[4,4,384,128]{3,2,1,0:T(8,128)} %copy.32), calls=%async_computation.7 | async-start | bytes 6291456 | tf_op jit(solution)/shard_map/all_to_all | solution.py:29
  442.9 23.9 %all-to-all-start.3 = ((f32[4,384,128]{2,1,0:T(8,128)}), f32[4,384,128]{2,1,0:T(8,128)}, u32[]{:S(2)}, u32[]{:S(2)}) async-start(f32[4,384,128]{2,1,0:T(8,128)} %reduce_sum.36), calls=%async_computation.3 | async-start | bytes 1572864 | tf_op jit(solution)/shard_map/all_to_all | solution.py:39
  448.2 49.3 %copy-start.55 = (f32[256]{0:T(256)S(1)}, f32[256]{0:T(256)}, u32[]{:S(2)}) copy-start(f32[256]{0:T(256)} %param.9) | copy-start | bytes 3076
  466.7 26.6 %all-to-all-start.7 = ((f32[4,384,128]{2,1,0:T(8,128)}), f32[4,384,128]{2,1,0:T(8,128)S(1)}, u32[]{:S(2)}, u32[]{:S(2)}) async-start(f32[4,384,128]{2,1,0:T(8,128)} %reduce_sum.38), calls=%async_computation.8 | async-start | bytes 1572864 | tf_op jit(solution)/shard_map/all_to_all | solution.py:39
  470.2 63.8 %all-reduce.2.cloned.1.call-start = ((), (), s32[]{:S(2)}) async-start(), calls=%async_computation.11 | async-start | bytes 1572864 | tf_op jit(solution)/shard_map/psum | solution.py:56
  494.1 41.2 %all-to-all-start.4 = ((f32[4,128,128]{2,1,0:T(8,128)}), f32[4,128,128]{2,1,0:T(8,128)S(1)}, u32[]{:S(2)}, u32[]{:S(2)}) async-start(f32[4,128,128]{2,1,0:T(8,128)} %broadcast_in_dim.10), calls=%async_computation.5 | async-start | bytes 524288 | tf_op jit(solution)/shard_map/all_to_all | solution.py:76
  497.5 48.3 %copy-start.54 = (f32[256,256]{1,0:T(8,128)S(1)}, f32[256,256]{1,0:T(8,128)}, u32[]{:S(2)}) copy-start(f32[256,256]{1,0:T(8,128)} %param.12) | copy-start | bytes 786436
  535.0 12.0 %copy-start.36 = (f32[384,512]{1,0:T(8,128)S(1)}, f32[384,512]{1,0:T(8,128)}, u32[]{:S(2)}) copy-start(f32[384,512]{1,0:T(8,128)} %all-reduce.2.cloned.1.call-done) | copy-start | bytes 2359300
  536.0 9.0 %all-to-all-start.8 = ((f32[4,128,128]{2,1,0:T(8,128)}), f32[4,128,128]{2,1,0:T(8,128)S(1)}, u32[]{:S(2)}, u32[]{:S(2)}) async-start(f32[4,128,128]{2,1,0:T(8,128)} %broadcast_in_dim.11), calls=%async_computation.9 | async-start | bytes 524288 | tf_op jit(solution)/shard_map/all_to_all | solution.py:76
  (36 other events, 100.5 us)
Sparse Core Ops, SparseCore 0:
  358.2 78.5 reduce-scatter.1
  473.4 60.5 all-reduce.1

commit v2 on v0

v2 whole, which is shorter than its diff:
```python
import functools

import jax
import jax.numpy as jnp
from jax import lax
from jax.experimental import pallas as pl
from jax.experimental.pallas import tpu as pltpu
from jax.sharding import PartitionSpec as P

HIGHEST = lax.Precision.HIGHEST
CUTS = (0.1875, 0.5625, 0.875, 1.0)
STEP = 16


def dot32(a, b):
    return jnp.dot(a, b, precision=HIGHEST, preferred_element_type=jnp.float32)


def dot_nt(a, b, precision=None):
    return lax.dot_general(a, b, (((1,), (1,)), ((), ())), precision=precision, preferred_element_type=jnp.float32)


def dot_nn(a, b):
    return jnp.dot(a, b, preferred_element_type=jnp.float32)


def split(v):
    high = lax.reduce_precision(v, 8, 7)
    return high.astype(jnp.bfloat16), (v - high).astype(jnp.bfloat16)


def after(x, earlier):
    return lax.optimization_barrier((x, earlier))[0]


def pick(x, i):
    return lax.dynamic_index_in_dim(x, i, axis=0, keepdims=False)


def turn_body(bounds, x_ref, *outs):
    for lo, hi, out in zip(bounds[:-1], bounds[1:], outs):
        out[0] = x_ref[:, lo:hi].T.astype(jnp.bfloat16)


def turn(x, bounds, blocks):
    depth, width = x.shape[0] // blocks, x.shape[1]
    sizes = [hi - lo for lo, hi in zip(bounds[:-1], bounds[1:])]
    return pl.pallas_call(
        functools.partial(turn_body, bounds),
        grid=(blocks,),
        in_specs=[pl.BlockSpec((depth, width), lambda i: (i, 0))],
        out_specs=[pl.BlockSpec((1, n, depth), lambda i: (i, 0, 0)) for n in sizes],
        out_shape=[jax.ShapeDtypeStruct((blocks, n, depth), jnp.bfloat16) for n in sizes],
        cost_estimate=pl.CostEstimate(flops=0, bytes_accessed=6 * x.size, transcendentals=0),
        name="turn",
    )(x)


def project_body(rows, order_ref, piece_ref, slab_ref, high_ref, low_ref, q_ref, *rest):
    outs, inner = rest[:rows], rest[rows]
    step = pl.program_id(0)

    @pl.when(step == 0)
    def _():
        piece = piece_ref[...]
        inner[...] = dot_nn(piece, high_ref[...]) + dot_nn(piece, low_ref[...])

    value = dot_nt(piece_ref[...], slab_ref[...]) - dot_nt(inner[...], q_ref[...], HIGHEST)
    for k in range(rows):
        @pl.when(step == k)
        def _():
            outs[k][...] = value


def project(order, piece, slab, high, low, q):
    rows = order.shape[0]
    count, depth = piece.shape
    mine, inner = slab.shape[0] // rows, q.shape[1]
    whole = lambda k, order: (0, 0)
    block = lambda k, order: (order[k], 0)
    return pl.pallas_call(
        functools.partial(project_body, rows),
        grid_spec=pltpu.PrefetchScalarGridSpec(
            num_scalar_prefetch=1,
            grid=(rows,),
            in_specs=[
                pl.BlockSpec((count, depth), whole),
                pl.BlockSpec((mine, depth), block),
                pl.BlockSpec((depth, inner), whole),
                pl.BlockSpec((depth, inner), whole),
                pl.BlockSpec((mine, inner), block),
            ],
            out_specs=[pl.BlockSpec((count, mine), whole)] * rows,
            scratch_shapes=[pltpu.VMEM((count, inner), jnp.float32)],
        ),
        out_shape=[jax.ShapeDtypeStruct((count, mine), jnp.float32)] * rows,
        cost_estimate=pl.CostEstimate(
            flops=2 * count * depth * (slab.shape[0] + 2 * inner) * 2,
            bytes_accessed=2 * (piece.size + slab.size + 2 * high.size) + 4 * count * slab.shape[0],
            transcendentals=0,
        ),
        name="project",
    )(order, piece, slab, high, low, q)


def make(rows, cols):
    half = cols // 2
    groups = [[i for i in range(cols) if i % 2 == core] for core in range(2)]

    def swap_core(x):
        return lax.ppermute(x, "col", [(i, i ^ 1) for i in range(cols)])

    def to_row(x, k):
        return lax.ppermute(x, "row", [(i, i ^ k) for i in range(rows)])

    def to_z(x, k):
        return lax.ppermute(x, "col", [(i, i ^ (2 * k)) for i in range(cols)])

    def row_sum(parts):
        got = [to_row(parts[k], k) for k in range(1, rows)]
        return sum(got, parts[0])

    def z_sum(parts):
        got = [to_z(parts[k], k) for k in range(1, half)]
        return sum(got, parts[0])

    def per_device(tokens, eigvecs, eigvals, v_first, v_second, t_first, t_second):
        nb = v_first.shape[1]
        row = lax.axis_index("row")
        core = lax.axis_index("col") % 2
        z = lax.axis_index("col") // 2
        width = eigvecs.shape[1]
        depth = v_first.shape[0]

        def in_core_order(mine, other, axis):
            return jnp.where(core == 0, jnp.concatenate([mine, other], axis), jnp.concatenate([other, mine], axis))

        raw = lax.all_to_all(tokens, ("row", "col"), split_axis=1, concat_axis=0, tiled=True)
        tok = raw.shape[0]
        mine = tok // rows
        v_own = jnp.concatenate([v_first, v_second], axis=1)
        v = in_core_order(v_own, swap_core(v_own), 0)
        v_high, v_low = split(v)
        gram = dot32(lax.dynamic_slice_in_dim(v[:, :nb], core * (nb // 2), nb // 2, 1).T, v[:, nb:])
        gram = gram.reshape(rows, nb // (4 * rows), 2 * nb)

        bounds = [0] + [min(width, -(-int(width * c) // STEP) * STEP) for c in CUTS]
        pieces = turn(eigvecs, bounds, half)
        raw, pieces, v_high, v_low, gram = lax.optimization_barrier((raw, pieces, v_high, v_low, gram))
        def send(piece, earlier):
            piece = after(piece, earlier)
            return lax.all_to_all(piece, "col", split_axis=0, concat_axis=0, tiled=True, axis_index_groups=groups)

        arrived = [send(pieces[0], raw)]
        slab = in_core_order(raw, swap_core(raw), 1)

        own = lax.dynamic_index_in_dim(slab.reshape(rows, 2, mine // 2, 2 * depth), core, 1, False)
        own = own.reshape(tok // 2, 2 * depth)
        along = (dot_nn(own, v_high) + dot_nn(own, v_low)).reshape(rows, mine // 2, 2 * nb)
        used = mine // 2 + gram.shape[1]
        pad = -used % (8 * half)
        packed = jnp.concatenate([along, gram, jnp.zeros((rows, pad, 2 * nb), jnp.float32)], axis=1)
        part = row_sum([pick(packed, row ^ k) for k in range(rows)]).reshape(half, (used + pad) // half, 2 * nb)
        total = z_sum([pick(part, z ^ k) for k in range(half)])
        got = jnp.stack([total] + [to_z(total, k) for k in range(1, half)])
        full = jnp.concatenate([pick(got, z ^ k) for k in range(half)], axis=0)
        earlier = full
        for piece in pieces[1:]:
            arrived.append(send(piece, (arrived[-1], earlier)))
            earlier = arrived[-1]
        both = jnp.stack([full] + [to_row(full, k) for k in range(1, rows)])
        both = jnp.stack([pick(both, row ^ k) for k in range(rows)])
        both_other = swap_core(both)
        gram = in_core_order(
            both[:, mine // 2: used].reshape(nb // 2, nb), both_other[:, mine // 2: used].reshape(nb // 2, nb), 0)
        along = in_core_order(both[:, : mine // 2], both_other[:, : mine // 2], 1).reshape(tok, 2 * nb)

        first = dot32(along[:, :nb], t_first)
        second = dot32(along[:, nb:] - dot32(first, gram), t_second)
        q = jnp.concatenate([first, second], axis=1)

        order = jnp.stack([row ^ k for k in range(rows)]).astype(jnp.int32)
        outs = []
        for piece in arrived:
            count = piece.shape[1]
            flat = piece.reshape(half * count, 2 * depth)
            part = row_sum(project(order, flat, slab, v_high, v_low, q))
            part = part.reshape(half, count, mine)
            outs.append(z_sum([pick(part, z ^ k) for k in range(half)]))
        return jnp.concatenate(outs, axis=0).T * lax.rsqrt(eigvals)[None, :]

    return per_device


def solution(mesh):
    in_specs = (
        P(("row", "col"), None),
        P("row", "col"),
        P("col"),
        P(("row", "col"), None),
        P(("row", "col"), None),
        P(),
        P(),
    )
    out_specs = P("row", "col")
    body = make(mesh.shape["row"], mesh.shape["col"])
    return jax.shard_map(body, mesh=mesh, in_specs=in_specs, out_specs=out_specs, check_vma=False)
```

time: 838 us -> 360 us (0.43)
  waiting for transfers between devices: 684 us -> 155 us
  matrix products: 93.9 us -> 11.7 us
  starting transfers between devices: 10.8 us -> 76.7 us
  Pallas kernels: 0 us -> 64.4 us
  other arithmetic: 0 us -> 32.8 us
  between operations: 13.2 us -> 0.56 us
  blocking collectives: 10.6 us -> 0 us
    psum x2 -> x0, waiting for transfers between devices: 274 us -> none  [per_device(): inner = lax.psum(partial_inner(panel, block), ('row', 'col'))]
    all_to_all x1 -> x4, waiting for transfers between devices: 292 us -> 28.7 us  [send(): lax.all_to_all(piece, 'col', split_axis=0, concat_axis=0, tiled=True, axi...]
    reduce_scatter x2 -> x0, waiting for transfers between devices: 118 us -> none  [the longest x1 88.4 us: per_device(): lax.psum_scatter(partial_value, 'col', scatter_dimension=1, tiled=True)]
    dot_general x7 -> x6, matrix products: 93.9 us -> 11.7 us  [the longest x4 7.89 us: dot32(): return jnp.dot(a, b, precision=HIGHEST, preferred_element_type=jnp.float32)]
    ppermute x0 -> x39, waiting for transfers between devices: none -> 80.5 us  [the longest x18 39.9 us: to_z(): return lax.ppermute(x, 'col', [(i, i ^ 2 * k) for i in range(cols)])]
    pallas_call x0 -> x5, Pallas kernels: none -> 64.4 us  [the longest x4 54 us: project(): pl.pallas_call(functools.partial(project_body, rows), grid_spec=pltpu.Pre...]
    ppermute x0 -> x39, starting transfers between devices: none -> 52.8 us  [the longest x18 32.1 us: to_z(): return lax.ppermute(x, 'col', [(i, i ^ 2 * k) for i in range(cols)])]
    all_to_all x1, waiting for transfers between devices: 0.01 us -> 45.5 us  [per_device(): lax.all_to_all(tokens, ('row', 'col'), split_axis=1, concat_axis=0, tiled...]
  transfers between devices with their start and end apart: 6 -> 44, of which waited for: 5 -> 21; matrix products, arithmetic and copies ran while one was open for 10% -> 15% of each run, Pallas kernels for 0% -> 18%
where the time goes in v2:
time: 360 us; the launch traced here: 359 us
  waiting for transfers between devices  155 us (43%)
  starting transfers between devices  76.7 us (21%)
  Pallas kernels  64.4 us (18%)
  other arithmetic  32.8 us (9%)
  local copies, waits for them, and re-layouts  18.2 us (5%)
  matrix products  11.7 us (3%)
    pallas_call x4, Pallas kernels, project(): pl.pallas_call(functools.partial(project_body, rows), grid_spec=pltpu.Pre...  54 us
    all_to_all x1, waiting for transfers between devices, per_device(): lax.all_to_all(tokens, ('row', 'col'), split_axis=1, concat_axis=0, tiled...  45.5 us
    ppermute x18, waiting for transfers between devices, to_z(): return lax.ppermute(x, 'col', [(i, i ^ 2 * k) for i in range(cols)])  39.9 us
    ppermute x18, waiting for transfers between devices, to_row(): return lax.ppermute(x, 'row', [(i, i ^ k) for i in range(rows)])  37.8 us
    ppermute x18, starting transfers between devices, to_z(): return lax.ppermute(x, 'col', [(i, i ^ 2 * k) for i in range(cols)])  32.1 us
    all_to_all x4, waiting for transfers between devices, send(): lax.all_to_all(piece, 'col', split_axis=0, concat_axis=0, tiled=True, axi...  28.7 us
    ppermute x18, starting transfers between devices, to_row(): return lax.ppermute(x, 'row', [(i, i ^ k) for i in range(rows)])  20.3 us
    all_to_all x4, starting transfers between devices, send(): lax.all_to_all(piece, 'col', split_axis=0, concat_axis=0, tiled=True, axi...  16.4 us
  transfers between devices with their start and end apart: 44, of which 21 were waited for; matrix products, arithmetic and copies ran while one was open for 15% of the time, Pallas kernels for 18%

profile of v2, /device:TPU:0, one launch (start us, length us, event | category | flops | bytes accessed | tf_op | source)
XLA Modules:
  0.0 359.0 jit_solution(7886231475931183915)
XLA Ops:
  0.0 4.0 %copy.30 = bf16[4,32,8,1664]{3,2,0,1:T(8,128)(2,1)} copy(bf16[4,32,8,1664]{3,2,1,0:T(8,128)(2,1)} %bitcast.114) | data formatting | bytes 6815744 | tf_op jit(solution)/shard_map/all_to_all | solution.py:138
  4.0 7.4 %all-to-all-start = ((bf16[32,32,1664]{2,0,1:T(8,128)(2,1)}), bf16[32,32,1664]{2,0,1:T(8,128)(2,1)}, u32[]{:S(2)}, u32[]{:S(2)}) async-start(bf16[32,32,1664]{2,0,1:T(8,128)(2,1)} %bitcast.111), calls=%async_computation | async-start | bytes 6815744 | tf_op jit(solution)/shard_map/all_to_all | solution.py:138
  15.1 10.4 %turn.1 = (bf16[4,48,3328]{2,1,0:T(8,128)(2,1)}, bf16[4,96,3328]{2,1,0:T(8,128)(2,1)}, bf16[4,80,3328]{2,1,0:T(8,128)(2,1)}, bf16[4,32,3328]{2,1,0:T(8,128)(2,1)}) custom-call(f32[13312,256]{1,0:T(8,128)} %x_ref.1), custom_call_target="tpu_custom_call" | custom-call | bytes 20447232 | tf_op jit(solution)/shard_map/turn/pallas_call | solution.py:48
  25.5 7.5 %fusion = (bf16[3328,512]{1,0:T(8,128)(2,1)}, f32[3328,512]{1,0:T(8,128)S(1)}) fusion(f32[1664,512]{1,0:T(8,128)} %constant_dynamic-update-slice_fusion, f32[1664,512]{1,0:T(8,128)} %collective-permute-done, pred[]{:T(512)S(6)} %eq.4), kind=kLoop, calls=%fused_computation.2 | loop fusion | flops 10223616 | bytes 17039360 | tf_op jit(solution)/shard_map/convert_element_type | solution.py:29
  38.9 5.2 %reduce-precision_convert_fusion.high_ref = bf16[3328,512]{1,0:T(8,128)(2,1)} fusion(f32[3328,512]{1,0:T(8,128)} %copy-done.2), kind=kLoop, calls=%fused_computation.1 | loop fusion | flops 3407872 | bytes 10223616 | tf_op jit(solution)/shard_map/convert_element_type | solution.py:29
  44.1 45.5 %all-to-all-done = bf16[32,32,1664]{2,0,1:T(8,128)(2,1)} async-done(((bf16[32,32,1664]{2,0,1:T(8,128)(2,1)}), bf16[32,32,1664]{2,0,1:T(8,128)(2,1)}, u32[]{:S(2)}, u32[]{:S(2)}) %all-to-all-start) | async-done | bytes 3407904 | tf_op jit(solution)/shard_map/all_to_all | solution.py:138
  89.6 3.5 all-to-all-start.1
  95.9 3.5 fusion.2
  108.5 8.2 %collective-permute-done.4 = f32[160,512]{1,0:T(8,128)S(1)} collective-permute-done((f32[160,512]{1,0:T(8,128)}, f32[160,512]{1,0:T(8,128)S(1)}, u32[]{:S(2)}, u32[]{:S(2)}) %collective-permute-start.4) | collective-permute-done | bytes 327712 | tf_op jit(solution)/shard_map/ppermute | solution.py:114
  116.7 6.2 %collective-permute-done.3 = f32[160,512]{1,0:T(8,128)} collective-permute-done((f32[160,512]{1,0:T(8,128)}, f32[160,512]{1,0:T(8,128)}, u32[]{:S(2)}, u32[]{:S(2)}) %collective-permute-start.3) | collective-permute-done | bytes 327712 | tf_op jit(solution)/shard_map/ppermute | solution.py:114
  125.4 3.3 collective-permute-start.5
  135.3 3.1 collective-permute-start.8
  143.8 4.7 %all-to-all-start.2 = ((bf16[4,96,3328]{2,1,0:T(8,128)(2,1)}), bf16[4,96,3328]{2,1,0:T(8,128)(2,1)}, u32[]{:S(2)}, u32[]{:S(2)}) async-start(bf16[4,96,3328]{2,1,0:T(8,128)(2,1)} %get-tuple-element.52), calls=%async_computation.2 | async-start | bytes 5111808 | tf_op jit(solution)/shard_map/all_to_all | solution.py:152
  152.1 8.0 %collective-permute-done.13 = f32[160,512]{1,0:T(8,128)S(1)} collective-permute-done((f32[160,512]{1,0:T(8,128)S(1)}, f32[160,512]{1,0:T(8,128)S(1)}, u32[]{:S(2)}, u32[]{:S(2)}) %collective-permute-start.13) | collective-permute-done | bytes 327712 | tf_op jit(solution)/shard_map/ppermute | solution.py:114
  160.1 6.0 %collective-permute-done.12 = f32[160,512]{1,0:T(8,128)S(1)} collective-permute-done((f32[160,512]{1,0:T(8,128)S(1)}, f32[160,512]{1,0:T(8,128)S(1)}, u32[]{:S(2)}, u32[]{:S(2)}) %collective-permute-start.12) | collective-permute-done | bytes 327712 | tf_op jit(solution)/shard_map/ppermute | solution.py:114
  167.2 9.2 %maximum_select_fusion.1.slab_ref = bf16[1024,3328]{1,0:T(8,128)(2,1)} fusion(bf16[1024,1664]{1,0:T(8,128)(2,1)} %collective-permute-done.1, bf16[1024,1664]{1,0:T(8,128)(2,1)} %bitcast.5, pred[]{:T(512)S(6)} %eq.4), kind=kLoop, calls=%fused_computation.4 | loop fusion | flops 30670848 | bytes 13631489 | tf_op jit(solution)/shard_map/jit(_where)/select_n | solution.py:136
  178.2 28.7 %all-to-all-done.2 = bf16[4,96,3328]{2,1,0:T(8,128)(2,1)} async-done(((bf16[4,96,3328]{2,1,0:T(8,128)(2,1)}), bf16[4,96,3328]{2,1,0:T(8,128)(2,1)}, u32[]{:S(2)}, u32[]{:S(2)}) %all-to-all-start.2) | async-done | bytes 2555936 | tf_op jit(solution)/shard_map/all_to_all | solution.py:152
  206.9 4.4 %all-to-all-start.3 = ((bf16[4,80,3328]{2,1,0:T(8,128)(2,1)}), bf16[4,80,3328]{2,1,0:T(8,128)(2,1)}, u32[]{:S(2)}, u32[]{:S(2)}) async-start(bf16[4,80,3328]{2,1,0:T(8,128)(2,1)} %get-tuple-element.58), calls=%async_computation.3 | async-start | bytes 4259840 | tf_op jit(solution)/shard_map/all_to_all | solution.py:152
  220.2 12.5 %project.4 = (f32[192,256]{1,0:T(8,128)}, f32[192,256]{1,0:T(8,128)}, f32[192,256]{1,0:T(8,128)}, f32[192,256]{1,0:T(8,128)}) custom-call(s32[4]{0:T(128)} %pad_add_fusion.order_ref, bf16[192,3328]{1,0:T(8,128)(2,1)} %bitcast.122, bf16[1024,3328]{1,0:T(8,128)(2,1)} %maximum_select_fusion.1.slab_ref, bf16[3328,512]{1,0:T(8,128)(2,1)} %reduce-precision_convert_fusion.high_ref, ...), custom_call_target="tpu_custom_call" | custom-call | flops 5234491392 | bytes 15695872 | tf_op jit(solution)/shard_map/project/pallas_call | solution.py:81
  236.2 5.4 %collective-permute-done.17 = f32[192,256]{1,0:T(8,128)S(1)} collective-permute-done((f32[192,256]{1,0:T(8,128)}, f32[192,256]{1,0:T(8,128)S(1)}, u32[]{:S(2)}, u32[]{:S(2)}) %collective-permute-start.17) | collective-permute-done | bytes 196640 | tf_op jit(solution)/shard_map/ppermute | solution.py:114
  245.0 15.4 %project.5 = (f32[384,256]{1,0:T(8,128)}, f32[384,256]{1,0:T(8,128)}, f32[384,256]{1,0:T(8,128)}, f32[384,256]{1,0:T(8,128)}) custom-call(s32[4]{0:T(128)} %pad_add_fusion.order_ref, bf16[384,3328]{1,0:T(8,128)(2,1)} %bitcast.38.piece_ref, bf16[1024,3328]{1,0:T(8,128)(2,1)} %maximum_select_fusion.1.slab_ref, ...), custom_call_target="tpu_custom_call" | custom-call | flops 10468982784 | bytes 17760256 | tf_op jit(solution)/shard_map/project/pallas_call | solution.py:81
  264.1 3.5 collective-permute-start.20
  267.9 4.2 %collective-permute-done.20 = f32[48,256]{0,1:T(8,128)S(1)} collective-permute-done((f32[48,256]{0,1:T(8,128)S(1)}, f32[48,256]{0,1:T(8,128)S(1)}, u32[]{:S(2)}, u32[]{:S(2)}) %collective-permute-start.20) | collective-permute-done | bytes 49184 | tf_op jit(solution)/shard_map/ppermute | solution.py:117
  272.1 4.8 %collective-permute-start.18 = (f32[48,256]{0,1:T(8,128)S(1)}, f32[48,256]{0,1:T(8,128)S(1)}, u32[]{:S(2)}, u32[]{:S(2)}) collective-permute-start(f32[48,256]{0,1:T(8,128)S(1)} %bitcast.137), channel_id=1, source_target_pairs={{0,2},{1,3},{2,0},{3,1},{4,6},{5,7},{6,4},{7,5},{8,10},{9,11},{10,... | collective-permute-start | bytes 147464 | tf_op jit(solution)/shard_map/ppermute | solution.py:117
  281.0 3.7 %all-to-all-start.4 = ((bf16[4,32,3328]{2,1,0:T(8,128)(2,1)}), bf16[4,32,3328]{2,1,0:T(8,128)(2,1)S(1)}, u32[]{:S(2)}, u32[]{:S(2)}) async-start(bf16[4,32,3328]{2,1,0:T(8,128)(2,1)} %get-tuple-element.64), calls=%async_computation.4 | async-start | bytes 1703936 | tf_op jit(solution)/shard_map/all_to_all | solution.py:152
  285.1 3.7 %collective-permute-start.26 = (f32[96,256]{0,1:T(8,128)S(1)}, f32[96,256]{0,1:T(8,128)S(1)}, u32[]{:S(2)}, u32[]{:S(2)}) collective-permute-start(f32[96,256]{0,1:T(8,128)S(1)} %bitcast.133), channel_id=1, source_target_pairs={{0,6},{1,7},{2,4},{3,5},{4,2},{5,3},{6,0},{7,1},{8,14},{9,15},{10,... | collective-permute-start | bytes 294920 | tf_op jit(solution)/shard_map/ppermute | solution.py:117
  289.9 14.0 %project.6 = (f32[320,256]{1,0:T(8,128)}, f32[320,256]{1,0:T(8,128)}, f32[320,256]{1,0:T(8,128)}, f32[320,256]{1,0:T(8,128)}) custom-call(s32[4]{0:T(128)} %pad_add_fusion.order_ref, bf16[320,3328]{1,0:T(8,128)(2,1)} %bitcast.44.piece_ref, bf16[1024,3328]{1,0:T(8,128)(2,1)} %maximum_select_fusion.1.slab_ref, ...), custom_call_target="tpu_custom_call" | custom-call | flops 8724152320 | bytes 17072128 | tf_op jit(solution)/shard_map/project/pallas_call | solution.py:81
  307.4 10.1 %collective-permute-done.25 = f32[96,256]{0,1:T(8,128)S(1)} collective-permute-done((f32[96,256]{0,1:T(8,128)S(1)}, f32[96,256]{0,1:T(8,128)S(1)}, u32[]{:S(2)}, u32[]{:S(2)}) %collective-permute-start.25) | collective-permute-done | bytes 98336 | tf_op jit(solution)/shard_map/ppermute | solution.py:117
  318.6 12.0 %project.7 = (f32[128,256]{1,0:T(8,128)}, f32[128,256]{1,0:T(8,128)}, f32[128,256]{1,0:T(8,128)}, f32[128,256]{1,0:T(8,128)}) custom-call(s32[4]{0:T(128)} %pad_add_fusion.order_ref, bf16[128,3328]{1,0:T(8,128)(2,1)} %bitcast.117, bf16[1024,3328]{1,0:T(8,128)(2,1)} %maximum_select_fusion.1.slab_ref, bf16[3328,512]{1,0:T(8,128)(2,1)} %reduce-precision_convert_fusion.high_ref, ...), custom_call_target="tpu_custom_call" | custom-call | flops 3489660928 | bytes 15007744 | tf_op jit(solution)/shard_map/project/pallas_call | solution.py:81
  342.5 5.0 %collective-permute-start.36 = (f32[32,256]{0,1:T(8,128)S(1)}, f32[32,256]{0,1:T(8,128)S(1)}, u32[]{:S(2)}, u32[]{:S(2)}) collective-permute-start(f32[32,256]{0,1:T(8,128)S(1)} %bitcast.135), channel_id=1, source_target_pairs={{0,2},{1,3},{2,0},{3,1},{4,6},{5,7},{6,4},{7,5},{8,10},{9,11},{10,... | collective-permute-start | bytes 98312 | tf_op jit(solution)/shard_map/ppermute | solution.py:117
  347.6 6.1 %collective-permute-done.31 = f32[80,256]{0,1:T(8,128)S(1)} collective-permute-done((f32[80,256]{0,1:T(8,128)S(1)}, f32[80,256]{0,1:T(8,128)S(1)}, u32[]{:S(2)}, u32[]{:S(2)}) %collective-permute-start.31) | collective-permute-done | bytes 81952 | tf_op jit(solution)/shard_map/ppermute | solution.py:117
  353.8 4.2 %collective-permute-done.37 = f32[32,256]{0,1:T(8,128)S(1)} collective-permute-done((f32[32,256]{0,1:T(8,128)S(1)}, f32[32,256]{0,1:T(8,128)S(1)}, u32[]{:S(2)}, u32[]{:S(2)}) %collective-permute-start.37) | collective-permute-done | bytes 32800 | tf_op jit(solution)/shard_map/ppermute | solution.py:117
  (155 shorter events, 84.4 us)
Async XLA Ops:
  4.0 85.6 %all-to-all-start = ((bf16[32,32,1664]{2,0,1:T(8,128)(2,1)}), bf16[32,32,1664]{2,0,1:T(8,128)(2,1)}, u32[]{:S(2)}, u32[]{:S(2)}) async-start(bf16[32,32,1664]{2,0,1:T(8,128)(2,1)} %bitcast.111), calls=%async_computation | async-start | bytes 6815744 | tf_op jit(solution)/shard_map/all_to_all | solution.py:138
  14.9 10.6 %collective-permute-start = (f32[1664,512]{1,0:T(8,128)}, f32[1664,512]{1,0:T(8,128)}, u32[]{:S(2)}, u32[]{:S(2)}) collective-permute-start(f32[1664,512]{1,0:T(8,128)} %constant_dynamic-update-slice_fusion), channel_id=1, source_target_pairs={{0,1},{1,0},{2,3},{3,2},{4,5},{5,4},{6,7},{7,6},{8,9},{9,8},{10,11... | collective-permute-start | bytes 10223624 | tf_op jit(solution)/shard_map/ppermute | solution.py:111
  89.6 54.1 %all-to-all-start.1 = ((bf16[4,48,3328]{2,1,0:T(8,128)(2,1)}), bf16[4,48,3328]{2,1,0:T(8,128)(2,1)S(1)}, u32[]{:S(2)}, u32[]{:S(2)}) async-start(bf16[4,48,3328]{2,1,0:T(8,128)(2,1)} %get-tuple-element.43), calls=%async_computation.1 | async-start | bytes 2555904 | tf_op jit(solution)/shard_map/all_to_all | solution.py:152
  105.0 11.7 %collective-permute-start.4 = (f32[160,512]{1,0:T(8,128)}, f32[160,512]{1,0:T(8,128)S(1)}, u32[]{:S(2)}, u32[]{:S(2)}) collective-permute-start(f32[160,512]{1,0:T(8,128)} %get-tuple-element.76), channel_id=1, source_target_pairs={{0,24},{8,16},{16,8},{24,0},{1,25},{9,17},{17,9},{25,1},{2,26},{10... | collective-permute-start | bytes 983048 | tf_op jit(solution)/shard_map/ppermute | solution.py:114
  106.0 17.0 %collective-permute-start.3 = (f32[160,512]{1,0:T(8,128)}, f32[160,512]{1,0:T(8,128)}, u32[]{:S(2)}, u32[]{:S(2)}) collective-permute-start(f32[160,512]{1,0:T(8,128)} %get-tuple-element.77), channel_id=1, source_target_pairs={{0,16},{8,24},{16,0},{24,8},{1,17},{9,25},{17,1},{25,9},{2,18},{10... | collective-permute-start | bytes 983048 | tf_op jit(solution)/shard_map/ppermute | solution.py:114
  107.4 15.5 %collective-permute-start.2 = (f32[160,512]{1,0:T(8,128)S(1)}, f32[160,512]{1,0:T(8,128)}, u32[]{:S(2)}, u32[]{:S(2)}) collective-permute-start(f32[160,512]{1,0:T(8,128)S(1)} %get-tuple-element.75), channel_id=1, source_target_pairs={{0,8},{8,0},{16,24},{24,16},{1,9},{9,1},{17,25},{25,17},{2,10},{10... | collective-permute-start | bytes 983048 | tf_op jit(solution)/shard_map/ppermute | solution.py:114
  143.8 63.1 %all-to-all-start.2 = ((bf16[4,96,3328]{2,1,0:T(8,128)(2,1)}), bf16[4,96,3328]{2,1,0:T(8,128)(2,1)}, u32[]{:S(2)}, u32[]{:S(2)}) async-start(bf16[4,96,3328]{2,1,0:T(8,128)(2,1)} %get-tuple-element.52), calls=%async_computation.2 | async-start | bytes 5111808 | tf_op jit(solution)/shard_map/all_to_all | solution.py:152
  148.5 11.6 %collective-permute-start.13 = (f32[160,512]{1,0:T(8,128)S(1)}, f32[160,512]{1,0:T(8,128)S(1)}, u32[]{:S(2)}, u32[]{:S(2)}) collective-permute-start(f32[160,512]{1,0:T(8,128)S(1)} %get-tuple-element.87), channel_id=1, source_target_pairs={{0,24},{8,16},{16,8},{24,0},{1,25},{9,17},{17,9},{25,1},{2,26},{10... | collective-permute-start | bytes 983048 | tf_op jit(solution)/shard_map/ppermute | solution.py:114
  149.9 16.2 %collective-permute-start.12 = (f32[160,512]{1,0:T(8,128)S(1)}, f32[160,512]{1,0:T(8,128)S(1)}, u32[]{:S(2)}, u32[]{:S(2)}) collective-permute-start(f32[160,512]{1,0:T(8,128)S(1)} %get-tuple-element.87), channel_id=1, source_target_pairs={{0,16},{8,24},{16,0},{24,8},{1,17},{9,25},{17,1},{25,9},{2,18},{10... | collective-permute-start | bytes 983048 | tf_op jit(solution)/shard_map/ppermute | solution.py:114
  150.6 15.5 %collective-permute-start.11 = (f32[160,512]{1,0:T(8,128)S(1)}, f32[160,512]{1,0:T(8,128)S(1)}, u32[]{:S(2)}, u32[]{:S(2)}) collective-permute-start(f32[160,512]{1,0:T(8,128)S(1)} %get-tuple-element.87), channel_id=1, source_target_pairs={{0,8},{8,0},{16,24},{24,16},{1,9},{9,1},{17,25},{25,17},{2,10},{10... | collective-permute-start | bytes 983048 | tf_op jit(solution)/shard_map/ppermute | solution.py:114
  166.5 10.1 %collective-permute-start.14 = (f32[4,160,512]{2,1,0:T(8,128)S(1)}, f32[4,160,512]{2,1,0:T(8,128)}, u32[]{:S(2)}, u32[]{:S(2)}) collective-permute-start(f32[4,160,512]{2,1,0:T(8,128)S(1)} %pad_maximum_fusion.2), channel_id=1, source_target_pairs={{0,1},{1,0},{2,3},{3,2},{4,5},{5,4},{6,7},{7,6},{8,9},{9,8},{10,11... | collective-permute-start | bytes 3932168 | tf_op jit(solution)/shard_map/ppermute | solution.py:111
  206.9 74.2 %all-to-all-start.3 = ((bf16[4,80,3328]{2,1,0:T(8,128)(2,1)}), bf16[4,80,3328]{2,1,0:T(8,128)(2,1)}, u32[]{:S(2)}, u32[]{:S(2)}) async-start(bf16[4,80,3328]{2,1,0:T(8,128)(2,1)} %get-tuple-element.58), calls=%async_computation.3 | async-start | bytes 4259840 | tf_op jit(solution)/shard_map/all_to_all | solution.py:152
  232.7 8.9 %collective-permute-start.17 = (f32[192,256]{1,0:T(8,128)}, f32[192,256]{1,0:T(8,128)S(1)}, u32[]{:S(2)}, u32[]{:S(2)}) collective-permute-start(f32[192,256]{1,0:T(8,128)} %get-tuple-element.50), channel_id=1, source_target_pairs={{0,24},{8,16},{16,8},{24,0},{1,25},{9,17},{17,9},{25,1},{2,26},{10... | collective-permute-start | bytes 589832 | tf_op jit(solution)/shard_map/ppermute | solution.py:114
  234.0 10.0 %collective-permute-start.16 = (f32[192,256]{1,0:T(8,128)}, f32[192,256]{1,0:T(8,128)S(1)}, u32[]{:S(2)}, u32[]{:S(2)}) collective-permute-start(f32[192,256]{1,0:T(8,128)} %get-tuple-element.49), channel_id=1, source_target_pairs={{0,16},{8,24},{16,0},{24,8},{1,17},{9,25},{17,1},{25,9},{2,18},{10... | collective-permute-start | bytes 589832 | tf_op jit(solution)/shard_map/ppermute | solution.py:114
  234.7 9.3 %collective-permute-start.15 = (f32[192,256]{1,0:T(8,128)}, f32[192,256]{1,0:T(8,128)S(1)}, u32[]{:S(2)}, u32[]{:S(2)}) collective-permute-start(f32[192,256]{1,0:T(8,128)} %get-tuple-element.48), channel_id=1, source_target_pairs={{0,8},{8,0},{16,24},{24,16},{1,9},{9,1},{17,25},{25,17},{2,10},{10... | collective-permute-start | bytes 589832 | tf_op jit(solution)/shard_map/ppermute | solution.py:114
  260.5 24.3 %collective-permute-start.23 = (f32[384,256]{1,0:T(8,128)}, f32[384,256]{1,0:T(8,128)S(1)}, u32[]{:S(2)}, u32[]{:S(2)}) collective-permute-start(f32[384,256]{1,0:T(8,128)} %get-tuple-element.56), channel_id=1, source_target_pairs={{0,24},{8,16},{16,8},{24,0},{1,25},{9,17},{17,9},{25,1},{2,26},{10... | collective-permute-start | bytes 1179656 | tf_op jit(solution)/shard_map/ppermute | solution.py:114
  261.8 23.0 %collective-permute-start.22 = (f32[384,256]{1,0:T(8,128)}, f32[384,256]{1,0:T(8,128)S(1)}, u32[]{:S(2)}, u32[]{:S(2)}) collective-permute-start(f32[384,256]{1,0:T(8,128)} %get-tuple-element.55), channel_id=1, source_target_pairs={{0,16},{8,24},{16,0},{24,8},{1,17},{9,25},{17,1},{25,9},{2,18},{10... | collective-permute-start | bytes 1179656 | tf_op jit(solution)/shard_map/ppermute | solution.py:114
  262.5 22.3 %collective-permute-start.21 = (f32[384,256]{1,0:T(8,128)}, f32[384,256]{1,0:T(8,128)S(1)}, u32[]{:S(2)}, u32[]{:S(2)}) collective-permute-start(f32[384,256]{1,0:T(8,128)} %get-tuple-element.54), channel_id=1, source_target_pairs={{0,8},{8,0},{16,24},{24,16},{1,9},{9,1},{17,25},{25,17},{2,10},{10... | collective-permute-start | bytes 1179656 | tf_op jit(solution)/shard_map/ppermute | solution.py:114
  267.7 10.7 %collective-permute-start.19 = (f32[48,256]{0,1:T(8,128)S(1)}, f32[48,256]{0,1:T(8,128)S(1)}, u32[]{:S(2)}, u32[]{:S(2)}) collective-permute-start(f32[48,256]{0,1:T(8,128)S(1)} %bitcast.136), channel_id=1, source_target_pairs={{0,4},{1,5},{2,6},{3,7},{4,0},{5,1},{6,2},{7,3},{8,12},{9,13},{10,... | collective-permute-start | bytes 147464 | tf_op jit(solution)/shard_map/ppermute | solution.py:117
  272.1 8.9 %collective-permute-start.18 = (f32[48,256]{0,1:T(8,128)S(1)}, f32[48,256]{0,1:T(8,128)S(1)}, u32[]{:S(2)}, u32[]{:S(2)}) collective-permute-start(f32[48,256]{0,1:T(8,128)S(1)} %bitcast.137), channel_id=1, source_target_pairs={{0,2},{1,3},{2,0},{3,1},{4,6},{5,7},{6,4},{7,5},{8,10},{9,11},{10,... | collective-permute-start | bytes 147464 | tf_op jit(solution)/shard_map/ppermute | solution.py:117
  281.0 36.6 %all-to-all-start.4 = ((bf16[4,32,3328]{2,1,0:T(8,128)(2,1)}), bf16[4,32,3328]{2,1,0:T(8,128)(2,1)S(1)}, u32[]{:S(2)}, u32[]{:S(2)}) async-start(bf16[4,32,3328]{2,1,0:T(8,128)(2,1)} %get-tuple-element.64), calls=%async_computation.4 | async-start | bytes 1703936 | tf_op jit(solution)/shard_map/all_to_all | solution.py:152
  285.1 21.7 %collective-permute-start.26 = (f32[96,256]{0,1:T(8,128)S(1)}, f32[96,256]{0,1:T(8,128)S(1)}, u32[]{:S(2)}, u32[]{:S(2)}) collective-permute-start(f32[96,256]{0,1:T(8,128)S(1)} %bitcast.133), channel_id=1, source_target_pairs={{0,6},{1,7},{2,4},{3,5},{4,2},{5,3},{6,0},{7,1},{8,14},{9,15},{10,... | collective-permute-start | bytes 294920 | tf_op jit(solution)/shard_map/ppermute | solution.py:117
  288.9 28.7 %collective-permute-start.25 = (f32[96,256]{0,1:T(8,128)S(1)}, f32[96,256]{0,1:T(8,128)S(1)}, u32[]{:S(2)}, u32[]{:S(2)}) collective-permute-start(f32[96,256]{0,1:T(8,128)S(1)} %bitcast.131), channel_id=1, source_target_pairs={{0,4},{1,5},{2,6},{3,7},{4,0},{5,1},{6,2},{7,3},{8,12},{9,13},{10,... | collective-permute-start | bytes 294920 | tf_op jit(solution)/shard_map/ppermute | solution.py:117
  289.0 28.5 %collective-permute-start.24 = (f32[96,256]{0,1:T(8,128)S(1)}, f32[96,256]{0,1:T(8,128)S(1)}, u32[]{:S(2)}, u32[]{:S(2)}) collective-permute-start(f32[96,256]{0,1:T(8,128)S(1)} %bitcast.134), channel_id=1, source_target_pairs={{0,2},{1,3},{2,0},{3,1},{4,6},{5,7},{6,4},{7,5},{8,10},{9,11},{10,... | collective-permute-start | bytes 294920 | tf_op jit(solution)/shard_map/ppermute | solution.py:117
  303.9 29.0 %collective-permute-start.29 = (f32[320,256]{1,0:T(8,128)}, f32[320,256]{1,0:T(8,128)S(1)}, u32[]{:S(2)}, u32[]{:S(2)}) collective-permute-start(f32[320,256]{1,0:T(8,128)} %get-tuple-element.62), channel_id=1, source_target_pairs={{0,24},{8,16},{16,8},{24,0},{1,25},{9,17},{17,9},{25,1},{2,26},{10... | collective-permute-start | bytes 983048 | tf_op jit(solution)/shard_map/ppermute | solution.py:114
  304.9 29.1 %collective-permute-start.28 = (f32[320,256]{1,0:T(8,128)}, f32[320,256]{1,0:T(8,128)S(1)}, u32[]{:S(2)}, u32[]{:S(2)}) collective-permute-start(f32[320,256]{1,0:T(8,128)} %get-tuple-element.61), channel_id=1, source_target_pairs={{0,16},{8,24},{16,0},{24,8},{1,17},{9,25},{17,1},{25,9},{2,18},{10... | collective-permute-start | bytes 983048 | tf_op jit(solution)/shard_map/ppermute | solution.py:114
  306.8 27.3 %collective-permute-start.27 = (f32[320,256]{1,0:T(8,128)}, f32[320,256]{1,0:T(8,128)S(1)}, u32[]{:S(2)}, u32[]{:S(2)}) collective-permute-start(f32[320,256]{1,0:T(8,128)} %get-tuple-element.60), channel_id=1, source_target_pairs={{0,8},{8,0},{16,24},{24,16},{1,9},{9,1},{17,25},{25,17},{2,10},{10... | collective-permute-start | bytes 983048 | tf_op jit(solution)/shard_map/ppermute | solution.py:114
  335.9 17.7 %collective-permute-start.31 = (f32[80,256]{0,1:T(8,128)S(1)}, f32[80,256]{0,1:T(8,128)S(1)}, u32[]{:S(2)}, u32[]{:S(2)}) collective-permute-start(f32[80,256]{0,1:T(8,128)S(1)} %bitcast.139), channel_id=1, source_target_pairs={{0,4},{1,5},{2,6},{3,7},{4,0},{5,1},{6,2},{7,3},{8,12},{9,13},{10,... | collective-permute-start | bytes 245768 | tf_op jit(solution)/shard_map/ppermute | solution.py:117
  337.6 16.0 %collective-permute-start.30 = (f32[80,256]{0,1:T(8,128)S(1)}, f32[80,256]{0,1:T(8,128)S(1)}, u32[]{:S(2)}, u32[]{:S(2)}) collective-permute-start(f32[80,256]{0,1:T(8,128)S(1)} %bitcast.141), channel_id=1, source_target_pairs={{0,2},{1,3},{2,0},{3,1},{4,6},{5,7},{6,4},{7,5},{8,10},{9,11},{10,... | collective-permute-start | bytes 245768 | tf_op jit(solution)/shard_map/ppermute | solution.py:117
  340.3 13.5 %collective-permute-start.38 = (f32[32,256]{0,1:T(8,128)S(1)}, f32[32,256]{0,1:T(8,128)S(1)}, u32[]{:S(2)}, u32[]{:S(2)}) collective-permute-start(f32[32,256]{0,1:T(8,128)S(1)} %bitcast.130), channel_id=1, source_target_pairs={{0,6},{1,7},{2,4},{3,5},{4,2},{5,3},{6,0},{7,1},{8,14},{9,15},{10,... | collective-permute-start | bytes 98312 | tf_op jit(solution)/shard_map/ppermute | solution.py:117
  341.9 16.2 %collective-permute-start.37 = (f32[32,256]{0,1:T(8,128)S(1)}, f32[32,256]{0,1:T(8,128)S(1)}, u32[]{:S(2)}, u32[]{:S(2)}) collective-permute-start(f32[32,256]{0,1:T(8,128)S(1)} %bitcast.132), channel_id=1, source_target_pairs={{0,4},{1,5},{2,6},{3,7},{4,0},{5,1},{6,2},{7,3},{8,12},{9,13},{10,... | collective-permute-start | bytes 98312 | tf_op jit(solution)/shard_map/ppermute | solution.py:117
  342.5 15.5 %collective-permute-start.36 = (f32[32,256]{0,1:T(8,128)S(1)}, f32[32,256]{0,1:T(8,128)S(1)}, u32[]{:S(2)}, u32[]{:S(2)}) collective-permute-start(f32[32,256]{0,1:T(8,128)S(1)} %bitcast.135), channel_id=1, source_target_pairs={{0,2},{1,3},{2,0},{3,1},{4,6},{5,7},{6,4},{7,5},{8,10},{9,11},{10,... | collective-permute-start | bytes 98312 | tf_op jit(solution)/shard_map/ppermute | solution.py:117
  (25 other events, 445.6 us)

commit v3 on v0

v3 whole, which is shorter than its diff:
```python
import functools

import jax
import jax.numpy as jnp
from jax import lax
from jax.experimental import pallas as pl
from jax.experimental.pallas import tpu as pltpu
from jax.sharding import PartitionSpec as P


HIGHEST = lax.Precision.HIGHEST
CUTS = (0.25, 0.375, 0.6875, 0.875, 1.0)
GROUPS = ((0, 1), (2,), (3,), (4,))
STEP = 16
KINDS = (jnp.float32, jnp.float32, jnp.float32)
VMEM = pl.BlockSpec(memory_space=pltpu.VMEM)
SMEM = pl.BlockSpec(memory_space=pltpu.SMEM)


def dot32(a, b):
    return jnp.dot(a, b, precision=HIGHEST, preferred_element_type=jnp.float32)


def dot_nt(a, b):
    return lax.dot_general(a, b, (((1,), (1,)), ((), ())), preferred_element_type=jnp.float32)


def dot_nn(a, b):
    return jnp.dot(a, b, preferred_element_type=jnp.float32)


def split(v):
    high = lax.reduce_precision(v, 8, 7)
    return high.astype(jnp.bfloat16), (v - high).astype(jnp.bfloat16)


def split_here(v):
    high = v.astype(jnp.bfloat16)
    return high, (v - high.astype(jnp.float32)).astype(jnp.bfloat16)


def after(x, earlier):
    return lax.optimization_barrier((x, earlier))[0]


def pick(x, i):
    return lax.dynamic_index_in_dim(x, i, axis=0, keepdims=False)


def turn_body(bounds, blocks, at_ref, x_ref, *outs):
    i = pl.program_id(0)
    for k in range(blocks):
        @pl.when(i == k)
        def _():
            for j, (lo, hi) in enumerate(zip(bounds[:-1], bounds[1:])):
                outs[j * blocks + k][0] = x_ref[:, lo:hi].T.astype(jnp.bfloat16)


def turn(at, x, bounds, blocks):
    depth, width = x.shape[0] // (2 * blocks), x.shape[1]
    sizes = [hi - lo for lo, hi in zip(bounds[:-1], bounds[1:])]

    def source(i, h, at):
        return (2 * lax.bitwise_xor(i, at[0]) + lax.bitwise_xor(h, at[1]), 0)

    def target(k):
        return lambda i, h, at: (jnp.clip(2 * (i - k) + h, 0, 1), 0, 0)

    outs = pl.pallas_call(
        functools.partial(turn_body, bounds, blocks),
        grid_spec=pltpu.PrefetchScalarGridSpec(
            num_scalar_prefetch=1,
            grid=(blocks, 2),
            in_specs=[pl.BlockSpec((depth, width), source)],
            out_specs=[pl.BlockSpec((1, n, depth), target(k)) for n in sizes for k in range(blocks)],
        ),
        out_shape=[jax.ShapeDtypeStruct((2, n, depth), jnp.bfloat16) for n in sizes for _ in range(blocks)],
        cost_estimate=pl.CostEstimate(flops=0, bytes_accessed=6 * x.size, transcendentals=0),
        name="turn",
    )(at, x)
    return [outs[j * blocks:(j + 1) * blocks] for j in range(len(sizes))]


def project_body(count_pieces, rows, last, order_ref, *refs):
    pieces, (raw, other, high, low, q) = refs[:count_pieces], refs[count_pieces:count_pieces + 5]
    outs = refs[count_pieces + 5:-5]
    piece_in, slab_in, v_in, q_in, sems = refs[-5:]
    _, depth = piece_in.shape[1:]
    starts = [0]
    for piece in pieces:
        starts.append(starts[-1] + piece.shape[1])
    mine = raw.shape[0] // rows
    count_in = [0]

    def stage(*moves):
        copies = []
        for source, target in moves:
            copies.append(pltpu.make_async_copy(source, target, sems.at[count_in[0]]))
            copies[-1].start()
            count_in[0] += 1
        return copies

    def slab(k):
        at = pl.ds(pl.multiple_of(order_ref[k] * mine, mine), mine)
        return stage((q.at[at], q_in.at[k]), (raw.at[at], slab_in.at[0, k]), (other.at[at], slab_in.at[1, k]))

    def wait(copies):
        for copy in copies:
            copy.wait()

    lead = stage(
        *[(p.at[h], piece_in.at[h, pl.ds(s, p.shape[1])]) for h in range(2) for p, s in zip(pieces, starts)],
        (high, v_in.at[0]))
    tail = stage((low, v_in.at[1]))
    wait(lead)
    ready = [slab(0)]
    own, rest = piece_in[0], piece_in[1]
    inner = dot_nn(own, v_in[0, :depth]) + dot_nn(rest, v_in[0, depth:])
    wait(tail)
    ready += [slab(k) for k in range(1, min(rows, 2))]
    inner = inner + dot_nn(own, v_in[1, :depth]) + dot_nn(rest, v_in[1, depth:])
    u_high, u_low = split_here(inner)
    for k in range(rows):
        wait(ready[k])
        if k + 2 < rows:
            ready.append(slab(k + 2))
        q_high, q_low = split_here(q_in[k])
        change = dot_nt(u_high, q_high) + dot_nt(u_high, q_low) + dot_nt(u_low, q_high)
        value = dot_nt(own, slab_in[0, k]) + dot_nt(rest, slab_in[1, k]) - change
        if not last:
            outs[k][...] = value.astype(outs[k].dtype)
            continue
        for i, (lo, hi) in enumerate(zip(starts[:-1], starts[1:])):
            outs[0][k, order_ref[rows + i]] = value[lo:hi].astype(outs[0].dtype)


def project(order, pieces, raw, other, high, low, q, rows, sent, last=False):
    _, count, depth = pieces[0].shape
    mine, inner = raw.shape[0] // rows, q.shape[1]
    size = sum(piece.shape[1] for piece in pieces)
    anywhere = pl.BlockSpec(memory_space=pl.ANY)
    if last:
        shapes = [jax.ShapeDtypeStruct((rows, len(pieces), count, mine), sent)]
    else:
        shapes = [jax.ShapeDtypeStruct((size, mine), jnp.float32 if k == 0 else sent) for k in range(rows)]
    return pl.pallas_call(
        functools.partial(project_body, len(pieces), rows, last),
        in_specs=[SMEM] + [anywhere] * (len(pieces) + 5),
        out_specs=[VMEM] * len(shapes),
        out_shape=shapes,
        scratch_shapes=[
            pltpu.VMEM((2, size, depth), jnp.bfloat16),
            pltpu.VMEM((2, rows, mine, depth), jnp.bfloat16),
            pltpu.VMEM((2, 2 * depth, inner), jnp.bfloat16),
            pltpu.VMEM((rows, mine, inner), jnp.float32),
            pltpu.SemaphoreType.DMA((2 * len(pieces) + 3 * rows + 2,)),
        ],
        cost_estimate=pl.CostEstimate(
            flops=4 * size * depth * (raw.shape[0] + 2 * inner),
            bytes_accessed=4 * (size * depth + raw.size + high.size) + 4 * size * raw.shape[0],
            transcendentals=0,
        ),
        name="project",
    )(order, *pieces, raw, other, high, low, q)


def make(rows, cols):
    half = cols // 2
    wide = [[r * cols + 2 * z + core for r in range(rows) for z in range(half)] for core in range(2)]

    def swap_core(x):
        return lax.ppermute(x, "col", [(i, i ^ 1) for i in range(cols)])

    def to_row(x, k):
        return lax.ppermute(x, "row", [(i, i ^ k) for i in range(rows)])

    def to_z(x, k):
        return lax.ppermute(x, "col", [(i, i ^ (2 * k)) for i in range(cols)])

    def row_sum(parts):
        got = [to_row(parts[k], k) for k in range(1, rows)]
        return sum((g.astype(jnp.float32) for g in got), parts[0])

    def z_sum(parts):
        got = []
        for k in range(1, half):
            got.append(to_z(parts[k], k))
        return sum((g.astype(jnp.float32) for g in got), parts[0])

    def per_device(tokens, eigvecs, eigvals, v_first, v_second, t_first, t_second):
        nb = v_first.shape[1]
        row = lax.axis_index("row")
        core = lax.axis_index("col") % 2
        z = lax.axis_index("col") // 2
        width = eigvecs.shape[1]

        raw = lax.all_to_all(tokens, ("row", "col"), split_axis=1, concat_axis=0, tiled=True)
        tok = raw.shape[0]
        mine = tok // rows
        part_rows = mine // 2
        gram_rows = nb // (4 * rows)
        v_own = jnp.concatenate([v_first, v_second], axis=1)
        v_rest = swap_core(v_own)
        v_high, v_low = split(jnp.concatenate([v_own, v_rest], axis=0))
        depth = v_own.shape[0]
        gram = dot32(v_first.T, v_second).reshape(2, rows, gram_rows, 2 * nb)

        bounds = [0] + [min(width, -(-int(width * c) // STEP) * STEP) for c in CUTS]
        pieces = turn(jnp.stack([z, core]).astype(jnp.int32), eigvecs, bounds, half)
        far = sorted(range(1, half), key=lambda k: -(k & (half // 2)))

        def send(j, earlier):
            piece, got = pieces[j], {}
            for k in far:
                got[k] = to_z(piece[k] if earlier is None else after(piece[k], earlier), k)
            return [piece[0]] + [got[k] for k in range(1, half)]

        raw, pieces, v_high, v_low, gram = lax.optimization_barrier((raw, pieces, v_high, v_low, gram))
        arrived = [send(0, raw)]
        other = swap_core(raw)

        along = dot_nn(raw, v_high[:depth]) + dot_nn(raw, v_low[:depth])
        along = jnp.swapaxes(along.reshape(rows, 2, part_rows, 2 * nb), 0, 1)
        used = part_rows + gram_rows
        pad = -used % (8 * half)
        packed = jnp.concatenate([along, gram], axis=2)
        packed = pick(packed, core) + swap_core(pick(packed, 1 - core))
        part = row_sum([pick(packed, row ^ k) for k in range(rows)])
        part = jnp.pad(part, ((0, pad), (0, 0))).reshape(half, (used + pad) // half, 2 * nb)
        total = z_sum([pick(part, z ^ k) for k in range(half)])
        arrived.append(send(1, part))
        got = [total]
        for k in range(1, half):
            got.append(to_z(total, k))
        got = jnp.stack(got)
        full = jnp.concatenate([pick(got, z ^ k) for k in range(half)], axis=0)
        arrived.append(send(2, full))
        both = [full]
        for k in range(1, rows):
            both.append(to_row(full, k))
        both = jnp.stack(both)
        both = jnp.stack([pick(both, row ^ k) for k in range(rows)])
        both_other = swap_core(both)

        def in_core_order(a, b, axis):
            return jnp.where(core == 0, jnp.concatenate([a, b], axis), jnp.concatenate([b, a], axis))

        gram = in_core_order(
            both[:, part_rows:used].reshape(nb // 2, nb), both_other[:, part_rows:used].reshape(nb // 2, nb), 0)
        along = in_core_order(both[:, :part_rows], both_other[:, :part_rows], 1).reshape(tok, 2 * nb)
        first = dot32(along[:, :nb], t_first)
        second = dot32(along[:, nb:] - dot32(first, gram), t_second)
        q = jnp.concatenate([first, second], axis=1)

        near = jnp.stack([row ^ k for k in range(rows)]).astype(jnp.int32)
        plain = jnp.concatenate([jnp.arange(rows), jnp.stack([z ^ k for k in range(half)])]).astype(jnp.int32)

        def chunk(g, order, sent, earlier, last=False):
            ready = q if earlier is None else after(q, earlier)
            flat = [piece for j in GROUPS[g] for piece in arrived[j]]
            return project(order, flat, raw, other, v_high, v_low, ready, rows, sent, last)

        def of_z(x, g):
            parts, at = [[] for _ in range(half)], 0
            for j in GROUPS[g]:
                n = bounds[j + 1] - bounds[j]
                for k in range(half):
                    parts[k].append(x[at:at + n])
                    at += n
            return [p[0] if len(p) == 1 else jnp.concatenate(p, axis=0) for p in parts]

        sums = []
        parts = None
        for g, sent in enumerate(KINDS):
            if g < 2:
                arrived.append(send(g + 3, parts or q))
            parts = chunk(g, near, sent, parts)
            sums.append(of_z(row_sum(parts), g))
        whole = [jnp.concatenate(p, axis=0) for p in zip(*sums)]
        last, = chunk(len(KINDS), plain, jnp.bfloat16, parts, True)
        last = last.reshape(rows * half, -1, mine)
        whole = z_sum(whole[:1] + [p.astype(jnp.bfloat16) for p in whole[1:]])
        last = lax.all_to_all(last, ("row", "col"), split_axis=0, concat_axis=0, tiled=True, axis_index_groups=wide)
        rest = jnp.sum(last.astype(jnp.float32), axis=0)
        return jnp.concatenate([whole, rest], axis=0).T * lax.rsqrt(eigvals)[None, :]

    return per_device


def solution(mesh):
    in_specs = (
        P(("row", "col"), None),
        P("row", "col"),
        P("col"),
        P(("row", "col"), None),
        P(("row", "col"), None),
        P(),
        P(),
    )
    out_specs = P("row", "col")
    body = make(mesh.shape["row"], mesh.shape["col"])

    return jax.shard_map(body, mesh=mesh, in_specs=in_specs, out_specs=out_specs, check_vma=False)
```

time: 838 us -> 372 us (0.44)
  waiting for transfers between devices: 684 us -> 170 us
  matrix products: 93.9 us -> 16.9 us
  starting transfers between devices: 10.8 us -> 82.5 us
  Pallas kernels: 0 us -> 70.3 us
  local copies, waits for them, and re-layouts: 25.3 us -> 12.2 us
  other arithmetic: 0 us -> 12.5 us
  between operations: 13.2 us -> 0.89 us
  blocking collectives: 10.6 us -> 0 us
    all_to_all x1, waiting for transfers between devices: 292 us -> 0.01 us  [per_device(): lax.all_to_all(last, ('row', 'col'), split_axis=0, concat_axis=0, tiled=T...]
    psum x2 -> x0, waiting for transfers between devices: 274 us -> none  [per_device(): inner = lax.psum(partial_inner(panel, block), ('row', 'col'))]
    ppermute x0 -> x43, waiting for transfers between devices: none -> 122 us  [the longest x24 73.6 us: to_z(): return lax.ppermute(x, 'col', [(i, i ^ 2 * k) for i in range(cols)])]
    reduce_scatter x2 -> x0, waiting for transfers between devices: 118 us -> none  [the longest x1 88.4 us: per_device(): lax.psum_scatter(partial_value, 'col', scatter_dimension=1, tiled=True)]
    dot_general x7 -> x6, matrix products: 93.9 us -> 16.9 us  [the longest x2 8.68 us: dot_nn(): return jnp.dot(a, b, preferred_element_type=jnp.float32)]
    pallas_call x0 -> x5, Pallas kernels: none -> 70.3 us  [the longest x4 54.8 us: project(): pl.pallas_call(functools.partial(project_body, len(pieces), rows, last),...]
    ppermute x0 -> x43, starting transfers between devices: none -> 68.8 us  [the longest x24 50.3 us: to_z(): return lax.ppermute(x, 'col', [(i, i ^ 2 * k) for i in range(cols)])]
    all_to_all x1, waiting for transfers between devices: 0.01 us -> 48.1 us  [per_device(): lax.all_to_all(tokens, ('row', 'col'), split_axis=1, concat_axis=0, tiled...]
  transfers between devices with their start and end apart: 6 -> 45, of which waited for: 5 -> 22; matrix products, arithmetic and copies ran while one was open for 10% -> 7% of each run, Pallas kernels for 0% -> 19%
where the time goes in v3:
time: 372 us; the launch traced here: 365 us
  waiting for transfers between devices  170 us (46%)
  starting transfers between devices  82.5 us (22%)
  Pallas kernels  70.3 us (19%)
  matrix products  16.9 us (5%)
  other arithmetic  12.5 us (3%)
  local copies, waits for them, and re-layouts  12.2 us (3%)
    ppermute x24, waiting for transfers between devices, to_z(): return lax.ppermute(x, 'col', [(i, i ^ 2 * k) for i in range(cols)])  73.6 us
    pallas_call x4, Pallas kernels, project(): pl.pallas_call(functools.partial(project_body, len(pieces), rows, last),...  54.8 us
    ppermute x24, starting transfers between devices, to_z(): return lax.ppermute(x, 'col', [(i, i ^ 2 * k) for i in range(cols)])  50.3 us
    all_to_all x1, waiting for transfers between devices, per_device(): lax.all_to_all(tokens, ('row', 'col'), split_axis=1, concat_axis=0, tiled...  48.1 us
    ppermute x15, waiting for transfers between devices, to_row(): return lax.ppermute(x, 'row', [(i, i ^ k) for i in range(rows)])  45 us
    ppermute x15, starting transfers between devices, to_row(): return lax.ppermute(x, 'row', [(i, i ^ k) for i in range(rows)])  18.2 us
    pallas_call x1, Pallas kernels, turn(): pl.pallas_call(functools.partial(turn_body, bounds, blocks), grid_spec=pl...  15.5 us
    dot_general x2, matrix products, dot_nn(): return jnp.dot(a, b, preferred_element_type=jnp.float32)  8.68 us
  transfers between devices with their start and end apart: 45, of which 22 were waited for; matrix products, arithmetic and copies ran while one was open for 7% of the time, Pallas kernels for 19%

profile of v3, /device:TPU:0, one launch (start us, length us, event | category | flops | bytes accessed | tf_op | source)
XLA Modules:
  0.0 365.1 jit_solution(3954722564535724821)
XLA Ops:
  0.0 4.1 %copy.20 = bf16[4,32,8,1664]{3,2,0,1:T(8,128)(2,1)} copy(bf16[4,32,8,1664]{3,2,1,0:T(8,128)(2,1)} %bitcast.83) | data formatting | bytes 6815744 | tf_op jit(solution)/shard_map/all_to_all | solution.py:197
  4.1 7.4 %all-to-all-start = ((bf16[32,32,1664]{2,0,1:T(8,128)(2,1)}), bf16[32,32,1664]{2,0,1:T(8,128)(2,1)}, u32[]{:S(2)}, u32[]{:S(2)}) async-start(bf16[32,32,1664]{2,0,1:T(8,128)(2,1)} %bitcast.78), calls=%async_computation | async-start | bytes 6815744 | tf_op jit(solution)/shard_map/all_to_all | solution.py:197
  15.1 4.3 %fusion.39 = f32[256,256]{1,0:T(8,128)S(1)} fusion(f32[1664,256]{1,0:T(8,128)S(1)} %copy-done.3, f32[1664,256]{1,0:T(8,128)} %param.11), kind=kOutput, calls=%fused_computation.82 | convolution fusion | flops 1308622848 | bytes 3670016 | tf_op jit(solution)/shard_map/dot_general | solution.py:21
  20.2 15.5 %turn.1 = (bf16[2,64,1664]{2,1,0:T(8,128)(2,1)}, bf16[2,64,1664]{2,1,0:T(8,128)(2,1)}, bf16[2,64,1664]{2,1,0:T(8,128)(2,1)}, bf16[2,64,1664]{2,1,0:T(8,128)(2,1)...) custom-call(s32[2]{0:T(128)} %pad_add_fusion.1.at_ref, ...), custom_call_target="tpu_custom_call" | custom-call | bytes 20447232 | tf_op jit(solution)/shard_map/turn/pallas_call | solution.py:69
  35.8 5.8 %fusion = (bf16[3328,512]{1,0:T(8,128)(2,1)}, bf16[3328,512]{1,0:T(8,128)(2,1)}) fusion(f32[1664,512]{1,0:T(8,128)} %collective-permute-done, f32[1664,512]{1,0:T(8,128)} %constant_dynamic-update-slice_fusion), kind=kLoop, calls=%fused_computation.2 | loop fusion | flops 8519680 | bytes 13631488 | tf_op jit(solution)/shard_map/convert_element_type | solution.py:34
  41.6 48.1 %all-to-all-done = bf16[32,32,1664]{2,0,1:T(8,128)(2,1)} async-done(((bf16[32,32,1664]{2,0,1:T(8,128)(2,1)}), bf16[32,32,1664]{2,0,1:T(8,128)(2,1)}, u32[]{:S(2)}, u32[]{:S(2)}) %all-to-all-start) | async-done | bytes 3407904 | tf_op jit(solution)/shard_map/all_to_all | solution.py:197
  89.7 4.7 %fusion.1 = f32[1024,512]{1,0:T(8,128)S(1)} fusion(bf16[1024,1664]{1,0:T(8,128)(2,1)} %bitcast.5.refs_8_.refs_4_, bf16[3328,512]{1,0:T(8,128)(2,1)} %get-tuple-element.110.refs_11_.refs_7_), kind=kOutput, calls=%fused_computation.11 | convolution fusion | flops 1744830464 | bytes 7208960 | tf_op jit(solution)/shard_map/dot_general | solution.py:29
  94.4 4.0 %fusion.5 = f32[1024,512]{1,0:T(8,128)S(1)} fusion(f32[1024,512]{1,0:T(8,128)S(1)} %fusion.1, bf16[1024,1664]{1,0:T(8,128)(2,1)} %bitcast.5.refs_8_.refs_4_, bf16[3328,512]{1,0:T(8,128)(2,1)S(1)} %copy-done.2), kind=kOutput, calls=%fused_computation.15 | convolution fusion | flops 1745354752 | bytes 9306112 | tf_op jit(solution)/shard_map/dot_general | solution.py:29
  99.5 3.2 collective-permute-done.4
  107.9 6.4 %collective-permute-done.5 = f32[144,512]{1,0:T(8,128)S(1)} collective-permute-done((f32[144,512]{1,0:T(8,128)S(1)}, f32[144,512]{1,0:T(8,128)S(1)}, u32[]{:S(2)}, u32[]{:S(2)}) %collective-permute-start.5) | collective-permute-done | bytes 294944 | tf_op jit(solution)/shard_map/ppermute | solution.py:175
  114.2 5.9 %collective-permute-done.7 = f32[144,512]{1,0:T(8,128)S(1)} collective-permute-done((f32[144,512]{1,0:T(8,128)S(1)}, f32[144,512]{1,0:T(8,128)S(1)}, u32[]{:S(2)}, u32[]{:S(2)}) %collective-permute-start.7) | collective-permute-done | bytes 294944 | tf_op jit(solution)/shard_map/ppermute | solution.py:175
  128.0 3.4 collective-permute-done.13
  133.0 2.9 collective-permute-start.15
  135.9 2.7 collective-permute-done.17
  144.2 8.0 %collective-permute-done.20 = f32[160,512]{1,0:T(8,128)S(1)} collective-permute-done((f32[160,512]{1,0:T(8,128)S(1)}, f32[160,512]{1,0:T(8,128)S(1)}, u32[]{:S(2)}, u32[]{:S(2)}) %collective-permute-start.20) | collective-permute-done | bytes 327712 | tf_op jit(solution)/shard_map/ppermute | solution.py:175
  152.2 5.9 %collective-permute-done.19 = f32[160,512]{1,0:T(8,128)S(1)} collective-permute-done((f32[160,512]{1,0:T(8,128)S(1)}, f32[160,512]{1,0:T(8,128)S(1)}, u32[]{:S(2)}, u32[]{:S(2)}) %collective-permute-start.19) | collective-permute-done | bytes 327712 | tf_op jit(solution)/shard_map/ppermute | solution.py:175
  161.2 3.1 collective-permute-start.1
  170.0 4.8 %collective-permute-done.3.refs_3_ = bf16[2,64,1664]{2,1,0:T(8,128)(2,1)} collective-permute-done((bf16[2,64,1664]{2,1,0:T(8,128)(2,1)}, bf16[2,64,1664]{2,1,0:T(8,128)(2,1)}, u32[]{:S(2)}, u32[]{:S(2)}) %collective-permute-start.3) | collective-permute-done | bytes 426016 | tf_op jit(solution)/shard_map/ppermute | solution.py:178
  174.8 15.7 %collective-permute-start.9 = (bf16[2,32,1664]{2,1,0:T(8,128)(2,1)}, bf16[2,32,1664]{2,1,0:T(8,128)(2,1)S(1)}, u32[]{:S(2)}, u32[]{:S(2)}) collective-permute-start(bf16[2,32,1664]{2,1,0:T(8,128)(2,1)} %get-tuple-element.114), channel_id=1, source_target_pairs={{0,4},{1,5},{2,6},{3,7},{4,0},{5,1},{6,2},{7,3},{8,12},{9,13},{10,... | collective-permute-start | bytes 638984 | tf_op jit(solution)/shard_map/ppermute | solution.py:178
  190.5 12.1 %collective-permute-done.2.refs_2_ = bf16[2,64,1664]{2,1,0:T(8,128)(2,1)} collective-permute-done((bf16[2,64,1664]{2,1,0:T(8,128)(2,1)S(1)}, bf16[2,64,1664]{2,1,0:T(8,128)(2,1)}, u32[]{:S(2)}, u32[]{:S(2)}) %collective-permute-start.2) | collective-permute-done | bytes 426016 | tf_op jit(solution)/shard_map/ppermute | solution.py:178
  207.9 14.9 %collective-permute-done.9.refs_6_ = bf16[2,32,1664]{2,1,0:T(8,128)(2,1)S(1)} collective-permute-done((bf16[2,32,1664]{2,1,0:T(8,128)(2,1)}, bf16[2,32,1664]{2,1,0:T(8,128)(2,1)S(1)}, u32[]{:S(2)}, u32[]{:S(2)}) %collective-permute-start.9) | collective-permute-done | bytes 213024 | tf_op jit(solution)/shard_map/ppermute | solution.py:178
  224.4 4.0 %collective-permute-start.31 = (bf16[2,48,1664]{2,1,0:T(8,128)(2,1)}, bf16[2,48,1664]{2,1,0:T(8,128)(2,1)S(1)}, u32[]{:S(2)}, u32[]{:S(2)}) collective-permute-start(bf16[2,48,1664]{2,1,0:T(8,128)(2,1)} %get-tuple-element.135), channel_id=1, source_target_pairs={{0,2},{1,3},{2,0},{3,1},{4,6},{5,7},{6,4},{7,5},{8,10},{9,11},{10,... | collective-permute-start | bytes 958472 | tf_op jit(solution)/shard_map/ppermute | solution.py:178
  229.4 16.6 %project.4 = (f32[384,256]{1,0:T(8,128)}, f32[384,256]{1,0:T(8,128)}, f32[384,256]{1,0:T(8,128)}, f32[384,256]{1,0:T(8,128)}) custom-call(s32[4]{0:T(128)} %pad_add_fusion.order_ref, bf16[2,64,1664]{2,1,0:T(8,128)(2,1)} %get-tuple-element.99.refs_0_, bf16[2,64,1664]{2,1,0:T(8,128)(2,1)} %collective-permute-done.1.refs_1_, ...), custom_call_target="tpu_custom_call" | custom-call | flops 5234491392 | bytes 17760256 | tf_op jit(solution)/shard_map/project/pallas_call | solution.py:146
  247.6 5.2 %collective-permute-start.40 = (bf16[2,32,1664]{2,1,0:T(8,128)(2,1)S(1)}, bf16[2,32,1664]{2,1,0:T(8,128)(2,1)S(1)}, u32[]{:S(2)}, u32[]{:S(2)}) collective-permute-start(bf16[2,32,1664]{2,1,0:T(8,128)(2,1)S(1)} %copy-done.20), channel_id=1, source_target_pairs={{0,2},{1,3},{2,0},{3,1},{4,6},{5,7},{6,4},{7,5},{8,10},{9,11},{10,... | collective-permute-start | bytes 638984 | tf_op jit(solution)/shard_map/ppermute | solution.py:178
  252.8 23.0 %collective-permute-done.26.refs_2_ = bf16[2,80,1664]{2,1,0:T(8,128)(2,1)} collective-permute-done((bf16[2,80,1664]{2,1,0:T(8,128)(2,1)}, bf16[2,80,1664]{2,1,0:T(8,128)(2,1)}, u32[]{:S(2)}, u32[]{:S(2)}) %collective-permute-start.26) | collective-permute-done | bytes 532512 | tf_op jit(solution)/shard_map/ppermute | solution.py:178
  275.7 14.3 %project.5 = (f32[320,256]{1,0:T(8,128)}, f32[320,256]{1,0:T(8,128)}, f32[320,256]{1,0:T(8,128)}, f32[320,256]{1,0:T(8,128)}) custom-call(s32[4]{0:T(128)} %pad_add_fusion.order_ref, bf16[2,80,1664]{2,1,0:T(8,128)(2,1)} %get-tuple-element.121.refs_0_, bf16[2,80,1664]{2,1,0:T(8,128)(2,1)} %collective-permute-done.25.refs_1_, ...), custom_call_target="tpu_custom_call" | custom-call | flops 4362076160 | bytes 17072128 | tf_op jit(solution)/shard_map/project/pallas_call | solution.py:146
  296.2 12.3 %project.6 = (f32[192,256]{1,0:T(8,128)}, f32[192,256]{1,0:T(8,128)}, f32[192,256]{1,0:T(8,128)}, f32[192,256]{1,0:T(8,128)}) custom-call(s32[4]{0:T(128)} %pad_add_fusion.order_ref, bf16[2,48,1664]{2,1,0:T(8,128)(2,1)} %get-tuple-element.133.refs_0_, bf16[2,48,1664]{2,1,0:T(8,128)(2,1)} %copy-done.9, bf16[2,48,1664]{2,1,0:T(8,128)(2,1)} %copy-done.10, ...), custom_call_target="tpu_custom_call" | custom-call | flops 2617245696 | bytes 15695872 | tf_op jit(solution)/shard_map/project/pallas_call | solution.py:146
  311.5 11.6 %project.7 = bf16[4,4,32,256]{3,2,1,0:T(8,128)(2,1)} custom-call(s32[8]{0:T(128)} %concatenate.61.order_ref, bf16[2,32,1664]{2,1,0:T(8,128)(2,1)} %get-tuple-element.145.refs_0_, bf16[2,32,1664]{2,1,0:T(8,128)(2,1)} %copy-done.13, bf16[2,32,1664]{2,1,0:T(8,128)(2,1)} %copy-done.14, bf16[2,32,1664]{2,1,0:T(8,128)(2,1)} %copy-done.15, ...), custom_call_target="tpu_custom_call" | custom-call | flops 1744830464 | bytes 15007744 | tf_op jit(solution)/shard_map/project/pallas_call | solution.py:146
  323.2 6.2 %all-to-all-start.1 = ((bf16[16,32,256]{2,1,0:T(8,128)(2,1)}), bf16[16,32,256]{2,1,0:T(8,128)(2,1)S(1)}, u32[]{:S(2)}, u32[]{:S(2)}) async-start(bf16[16,32,256]{2,1,0:T(8,128)(2,1)} %bitcast.86), calls=%async_computation.1 | async-start | bytes 524288 | tf_op jit(solution)/shard_map/all_to_all | solution.py:283
  333.1 6.7 %collective-permute-done.34 = f32[192,256]{1,0:T(8,128)S(1)} collective-permute-done((f32[192,256]{1,0:T(8,128)}, f32[192,256]{1,0:T(8,128)S(1)}, u32[]{:S(2)}, u32[]{:S(2)}) %collective-permute-start.34) | collective-permute-done | bytes 196640 | tf_op jit(solution)/shard_map/ppermute | solution.py:175
  341.5 9.4 %collective-permute-done.35 = f32[192,256]{1,0:T(8,128)S(1)} collective-permute-done((f32[192,256]{1,0:T(8,128)}, f32[192,256]{1,0:T(8,128)S(1)}, u32[]{:S(2)}, u32[]{:S(2)}) %collective-permute-start.35) | collective-permute-done | bytes 196640 | tf_op jit(solution)/shard_map/ppermute | solution.py:175
  356.6 6.9 %collective-permute-done.38 = bf16[224,256]{1,0:T(8,128)(2,1)S(1)} collective-permute-done((bf16[224,256]{1,0:T(8,128)(2,1)S(1)}, bf16[224,256]{1,0:T(8,128)(2,1)S(1)}, u32[]{:S(2)}, u32[]{:S(2)}) %collective-permute-start.38) | collective-permute-done | bytes 114720 | tf_op jit(solution)/shard_map/ppermute | solution.py:178
  (163 shorter events, 64.9 us)
Async XLA Ops:
  4.1 85.6 %all-to-all-start = ((bf16[32,32,1664]{2,0,1:T(8,128)(2,1)}), bf16[32,32,1664]{2,0,1:T(8,128)(2,1)}, u32[]{:S(2)}, u32[]{:S(2)}) async-start(bf16[32,32,1664]{2,0,1:T(8,128)(2,1)} %bitcast.78), calls=%async_computation | async-start | bytes 6815744 | tf_op jit(solution)/shard_map/all_to_all | solution.py:197
  15.0 20.8 %collective-permute-start = (f32[1664,512]{1,0:T(8,128)}, f32[1664,512]{1,0:T(8,128)}, u32[]{:S(2)}, u32[]{:S(2)}) collective-permute-start(f32[1664,512]{1,0:T(8,128)} %constant_dynamic-update-slice_fusion), channel_id=1, source_target_pairs={{0,1},{1,0},{2,3},{3,2},{4,5},{5,4},{6,7},{7,6},{8,9},{9,8},{10,11... | collective-permute-start | bytes 10223624 | tf_op jit(solution)/shard_map/ppermute | solution.py:172
  105.4 14.7 %collective-permute-start.7 = (f32[144,512]{1,0:T(8,128)S(1)}, f32[144,512]{1,0:T(8,128)S(1)}, u32[]{:S(2)}, u32[]{:S(2)}) collective-permute-start(f32[144,512]{1,0:T(8,128)S(1)} %get-tuple-element.166), channel_id=1, source_target_pairs={{0,24},{8,16},{16,8},{24,0},{1,25},{9,17},{17,9},{25,1},{2,26},{10... | collective-permute-start | bytes 884744 | tf_op jit(solution)/shard_map/ppermute | solution.py:175
  106.4 15.0 %collective-permute-start.6 = (f32[144,512]{1,0:T(8,128)S(1)}, f32[144,512]{1,0:T(8,128)S(1)}, u32[]{:S(2)}, u32[]{:S(2)}) collective-permute-start(f32[144,512]{1,0:T(8,128)S(1)} %get-tuple-element.167), channel_id=1, source_target_pairs={{0,16},{8,24},{16,0},{24,8},{1,17},{9,25},{17,1},{25,9},{2,18},{10... | collective-permute-start | bytes 884744 | tf_op jit(solution)/shard_map/ppermute | solution.py:175
  135.9 92.4 %collective-permute-start.11 = (bf16[1024,1664]{1,0:T(8,128)(2,1)}, bf16[1024,1664]{1,0:T(8,128)(2,1)}, u32[]{:S(2)}, u32[]{:S(2)}) collective-permute-start(bf16[1024,1664]{1,0:T(8,128)(2,1)} %bitcast.5.refs_8_.refs_4_), channel_id=1, source_target_pairs={{0,1},{1,0},{2,3},{3,2},{4,5},{5,4},{6,7},{7,6},{8,9},{9,8},{10,11... | collective-permute-start | bytes 10223624 | tf_op jit(solution)/shard_map/ppermute | solution.py:172
  140.6 11.6 %collective-permute-start.20 = (f32[160,512]{1,0:T(8,128)S(1)}, f32[160,512]{1,0:T(8,128)S(1)}, u32[]{:S(2)}, u32[]{:S(2)}) collective-permute-start(f32[160,512]{1,0:T(8,128)S(1)} %get-tuple-element.169), channel_id=1, source_target_pairs={{0,24},{8,16},{16,8},{24,0},{1,25},{9,17},{17,9},{25,1},{2,26},{10... | collective-permute-start | bytes 983048 | tf_op jit(solution)/shard_map/ppermute | solution.py:175
  142.6 15.6 %collective-permute-start.19 = (f32[160,512]{1,0:T(8,128)S(1)}, f32[160,512]{1,0:T(8,128)S(1)}, u32[]{:S(2)}, u32[]{:S(2)}) collective-permute-start(f32[160,512]{1,0:T(8,128)S(1)} %get-tuple-element.169), channel_id=1, source_target_pairs={{0,16},{8,24},{16,0},{24,8},{1,17},{9,25},{17,1},{25,9},{2,18},{10... | collective-permute-start | bytes 983048 | tf_op jit(solution)/shard_map/ppermute | solution.py:175
  143.0 15.1 %collective-permute-start.18 = (f32[160,512]{1,0:T(8,128)S(1)}, f32[160,512]{1,0:T(8,128)S(1)}, u32[]{:S(2)}, u32[]{:S(2)}) collective-permute-start(f32[160,512]{1,0:T(8,128)S(1)} %get-tuple-element.169), channel_id=1, source_target_pairs={{0,8},{8,0},{16,24},{24,16},{1,9},{9,1},{17,25},{25,17},{2,10},{10... | collective-permute-start | bytes 983048 | tf_op jit(solution)/shard_map/ppermute | solution.py:175
  159.9 14.9 %collective-permute-start.3 = (bf16[2,64,1664]{2,1,0:T(8,128)(2,1)}, bf16[2,64,1664]{2,1,0:T(8,128)(2,1)}, u32[]{:S(2)}, u32[]{:S(2)}) collective-permute-start(bf16[2,64,1664]{2,1,0:T(8,128)(2,1)} %get-tuple-element.106), channel_id=1, source_target_pairs={{0,6},{1,7},{2,4},{3,5},{4,2},{5,3},{6,0},{7,1},{8,14},{9,15},{10,... | collective-permute-start | bytes 1277960 | tf_op jit(solution)/shard_map/ppermute | solution.py:178
  161.2 41.5 %collective-permute-start.2 = (bf16[2,64,1664]{2,1,0:T(8,128)(2,1)S(1)}, bf16[2,64,1664]{2,1,0:T(8,128)(2,1)}, u32[]{:S(2)}, u32[]{:S(2)}) collective-permute-start(bf16[2,64,1664]{2,1,0:T(8,128)(2,1)S(1)} %copy-done.18), channel_id=1, source_target_pairs={{0,4},{1,5},{2,6},{3,7},{4,0},{5,1},{6,2},{7,3},{8,12},{9,13},{10,... | collective-permute-start | bytes 1277960 | tf_op jit(solution)/shard_map/ppermute | solution.py:178
  161.2 45.3 %collective-permute-start.1 = (bf16[2,64,1664]{2,1,0:T(8,128)(2,1)}, bf16[2,64,1664]{2,1,0:T(8,128)(2,1)}, u32[]{:S(2)}, u32[]{:S(2)}) collective-permute-start(bf16[2,64,1664]{2,1,0:T(8,128)(2,1)} %get-tuple-element.102), channel_id=1, source_target_pairs={{0,2},{1,3},{2,0},{3,1},{4,6},{5,7},{6,4},{7,5},{8,10},{9,11},{10,... | collective-permute-start | bytes 1277960 | tf_op jit(solution)/shard_map/ppermute | solution.py:178
  164.4 43.5 %collective-permute-start.8 = (bf16[2,32,1664]{2,1,0:T(8,128)(2,1)}, bf16[2,32,1664]{2,1,0:T(8,128)(2,1)}, u32[]{:S(2)}, u32[]{:S(2)}) collective-permute-start(bf16[2,32,1664]{2,1,0:T(8,128)(2,1)} %get-tuple-element.112), channel_id=1, source_target_pairs={{0,2},{1,3},{2,0},{3,1},{4,6},{5,7},{6,4},{7,5},{8,10},{9,11},{10,... | collective-permute-start | bytes 638984 | tf_op jit(solution)/shard_map/ppermute | solution.py:178
  174.8 48.0 %collective-permute-start.9 = (bf16[2,32,1664]{2,1,0:T(8,128)(2,1)}, bf16[2,32,1664]{2,1,0:T(8,128)(2,1)S(1)}, u32[]{:S(2)}, u32[]{:S(2)}) collective-permute-start(bf16[2,32,1664]{2,1,0:T(8,128)(2,1)} %get-tuple-element.114), channel_id=1, source_target_pairs={{0,4},{1,5},{2,6},{3,7},{4,0},{5,1},{6,2},{7,3},{8,12},{9,13},{10,... | collective-permute-start | bytes 638984 | tf_op jit(solution)/shard_map/ppermute | solution.py:178
  202.7 21.7 %collective-permute-start.10 = (bf16[2,32,1664]{2,1,0:T(8,128)(2,1)}, bf16[2,32,1664]{2,1,0:T(8,128)(2,1)}, u32[]{:S(2)}, u32[]{:S(2)}) collective-permute-start(bf16[2,32,1664]{2,1,0:T(8,128)(2,1)} %get-tuple-element.116), channel_id=1, source_target_pairs={{0,6},{1,7},{2,4},{3,5},{4,2},{5,3},{6,0},{7,1},{8,14},{9,15},{10,... | collective-permute-start | bytes 638984 | tf_op jit(solution)/shard_map/ppermute | solution.py:178
  206.4 39.6 %collective-permute-start.27 = (bf16[2,80,1664]{2,1,0:T(8,128)(2,1)}, bf16[2,80,1664]{2,1,0:T(8,128)(2,1)S(1)}, u32[]{:S(2)}, u32[]{:S(2)}) collective-permute-start(bf16[2,80,1664]{2,1,0:T(8,128)(2,1)} %get-tuple-element.127), channel_id=1, source_target_pairs={{0,6},{1,7},{2,4},{3,5},{4,2},{5,3},{6,0},{7,1},{8,14},{9,15},{10,... | collective-permute-start | bytes 1597448 | tf_op jit(solution)/shard_map/ppermute | solution.py:178
  207.9 39.7 %collective-permute-start.25 = (bf16[2,80,1664]{2,1,0:T(8,128)(2,1)}, bf16[2,80,1664]{2,1,0:T(8,128)(2,1)}, u32[]{:S(2)}, u32[]{:S(2)}) collective-permute-start(bf16[2,80,1664]{2,1,0:T(8,128)(2,1)} %get-tuple-element.123), channel_id=1, source_target_pairs={{0,2},{1,3},{2,0},{3,1},{4,6},{5,7},{6,4},{7,5},{8,10},{9,11},{10,... | collective-permute-start | bytes 1597448 | tf_op jit(solution)/shard_map/ppermute | solution.py:178
  222.8 53.0 %collective-permute-start.26 = (bf16[2,80,1664]{2,1,0:T(8,128)(2,1)}, bf16[2,80,1664]{2,1,0:T(8,128)(2,1)}, u32[]{:S(2)}, u32[]{:S(2)}) collective-permute-start(bf16[2,80,1664]{2,1,0:T(8,128)(2,1)} %get-tuple-element.125), channel_id=1, source_target_pairs={{0,4},{1,5},{2,6},{3,7},{4,0},{5,1},{6,2},{7,3},{8,12},{9,13},{10,... | collective-permute-start | bytes 1597448 | tf_op jit(solution)/shard_map/ppermute | solution.py:178
  224.4 66.8 %collective-permute-start.31 = (bf16[2,48,1664]{2,1,0:T(8,128)(2,1)}, bf16[2,48,1664]{2,1,0:T(8,128)(2,1)S(1)}, u32[]{:S(2)}, u32[]{:S(2)}) collective-permute-start(bf16[2,48,1664]{2,1,0:T(8,128)(2,1)} %get-tuple-element.135), channel_id=1, source_target_pairs={{0,2},{1,3},{2,0},{3,1},{4,6},{5,7},{6,4},{7,5},{8,10},{9,11},{10,... | collective-permute-start | bytes 958472 | tf_op jit(solution)/shard_map/ppermute | solution.py:178
  228.4 64.1 %collective-permute-start.32 = (bf16[2,48,1664]{2,1,0:T(8,128)(2,1)}, bf16[2,48,1664]{2,1,0:T(8,128)(2,1)S(1)}, u32[]{:S(2)}, u32[]{:S(2)}) collective-permute-start(bf16[2,48,1664]{2,1,0:T(8,128)(2,1)} %get-tuple-element.137), channel_id=1, source_target_pairs={{0,4},{1,5},{2,6},{3,7},{4,0},{5,1},{6,2},{7,3},{8,12},{9,13},{10,... | collective-permute-start | bytes 958472 | tf_op jit(solution)/shard_map/ppermute | solution.py:178
  246.0 47.6 %collective-permute-start.33 = (bf16[2,48,1664]{2,1,0:T(8,128)(2,1)S(1)}, bf16[2,48,1664]{2,1,0:T(8,128)(2,1)S(1)}, u32[]{:S(2)}, u32[]{:S(2)}) collective-permute-start(bf16[2,48,1664]{2,1,0:T(8,128)(2,1)S(1)} %copy-done.19), channel_id=1, source_target_pairs={{0,6},{1,7},{2,4},{3,5},{4,2},{5,3},{6,0},{7,1},{8,14},{9,15},{10,... | collective-permute-start | bytes 958472 | tf_op jit(solution)/shard_map/ppermute | solution.py:178
  247.6 46.0 %collective-permute-start.40 = (bf16[2,32,1664]{2,1,0:T(8,128)(2,1)S(1)}, bf16[2,32,1664]{2,1,0:T(8,128)(2,1)S(1)}, u32[]{:S(2)}, u32[]{:S(2)}) collective-permute-start(bf16[2,32,1664]{2,1,0:T(8,128)(2,1)S(1)} %copy-done.20), channel_id=1, source_target_pairs={{0,2},{1,3},{2,0},{3,1},{4,6},{5,7},{6,4},{7,5},{8,10},{9,11},{10,... | collective-permute-start | bytes 638984 | tf_op jit(solution)/shard_map/ppermute | solution.py:178
  290.0 39.4 %collective-permute-start.28 = (f32[320,256]{1,0:T(8,128)}, f32[320,256]{1,0:T(8,128)S(1)}, u32[]{:S(2)}, u32[]{:S(2)}) collective-permute-start(f32[320,256]{1,0:T(8,128)} %get-tuple-element.130), channel_id=1, source_target_pairs={{0,8},{8,0},{16,24},{24,16},{1,9},{9,1},{17,25},{25,17},{2,10},{10... | collective-permute-start | bytes 983048 | tf_op jit(solution)/shard_map/ppermute | solution.py:175
  291.1 40.3 %collective-permute-start.29 = (f32[320,256]{1,0:T(8,128)}, f32[320,256]{1,0:T(8,128)S(1)}, u32[]{:S(2)}, u32[]{:S(2)}) collective-permute-start(f32[320,256]{1,0:T(8,128)} %get-tuple-element.131), channel_id=1, source_target_pairs={{0,16},{8,24},{16,0},{24,8},{1,17},{9,25},{17,1},{25,9},{2,18},{10... | collective-permute-start | bytes 983048 | tf_op jit(solution)/shard_map/ppermute | solution.py:175
  292.4 40.4 %collective-permute-start.30 = (f32[320,256]{1,0:T(8,128)}, f32[320,256]{1,0:T(8,128)S(1)}, u32[]{:S(2)}, u32[]{:S(2)}) collective-permute-start(f32[320,256]{1,0:T(8,128)} %get-tuple-element.132), channel_id=1, source_target_pairs={{0,24},{8,16},{16,8},{24,0},{1,25},{9,17},{17,9},{25,1},{2,26},{10... | collective-permute-start | bytes 983048 | tf_op jit(solution)/shard_map/ppermute | solution.py:175
  293.6 15.6 %collective-permute-start.41 = (bf16[2,32,1664]{2,1,0:T(8,128)(2,1)}, bf16[2,32,1664]{2,1,0:T(8,128)(2,1)S(1)}, u32[]{:S(2)}, u32[]{:S(2)}) collective-permute-start(bf16[2,32,1664]{2,1,0:T(8,128)(2,1)} %get-tuple-element.149), channel_id=1, source_target_pairs={{0,4},{1,5},{2,6},{3,7},{4,0},{5,1},{6,2},{7,3},{8,12},{9,13},{10,... | collective-permute-start | bytes 638984 | tf_op jit(solution)/shard_map/ppermute | solution.py:178
  293.6 16.7 %collective-permute-start.42 = (bf16[2,32,1664]{2,1,0:T(8,128)(2,1)}, bf16[2,32,1664]{2,1,0:T(8,128)(2,1)S(1)}, u32[]{:S(2)}, u32[]{:S(2)}) collective-permute-start(bf16[2,32,1664]{2,1,0:T(8,128)(2,1)} %get-tuple-element.151), channel_id=1, source_target_pairs={{0,6},{1,7},{2,4},{3,5},{4,2},{5,3},{6,0},{7,1},{8,14},{9,15},{10,... | collective-permute-start | bytes 638984 | tf_op jit(solution)/shard_map/ppermute | solution.py:178
  309.2 41.8 %collective-permute-start.22 = (f32[384,256]{1,0:T(8,128)}, f32[384,256]{1,0:T(8,128)S(1)}, u32[]{:S(2)}, u32[]{:S(2)}) collective-permute-start(f32[384,256]{1,0:T(8,128)} %get-tuple-element.118), channel_id=1, source_target_pairs={{0,8},{8,0},{16,24},{24,16},{1,9},{9,1},{17,25},{25,17},{2,10},{10... | collective-permute-start | bytes 1179656 | tf_op jit(solution)/shard_map/ppermute | solution.py:175
  310.3 40.7 %collective-permute-start.23 = (f32[384,256]{1,0:T(8,128)}, f32[384,256]{1,0:T(8,128)S(1)}, u32[]{:S(2)}, u32[]{:S(2)}) collective-permute-start(f32[384,256]{1,0:T(8,128)} %get-tuple-element.119), channel_id=1, source_target_pairs={{0,16},{8,24},{16,0},{24,8},{1,17},{9,25},{17,1},{25,9},{2,18},{10... | collective-permute-start | bytes 1179656 | tf_op jit(solution)/shard_map/ppermute | solution.py:175
  323.2 40.7 %all-to-all-start.1 = ((bf16[16,32,256]{2,1,0:T(8,128)(2,1)}), bf16[16,32,256]{2,1,0:T(8,128)(2,1)S(1)}, u32[]{:S(2)}, u32[]{:S(2)}) async-start(bf16[16,32,256]{2,1,0:T(8,128)(2,1)} %bitcast.86), calls=%async_computation.1 | async-start | bytes 524288 | tf_op jit(solution)/shard_map/all_to_all | solution.py:283
  331.4 19.5 %collective-permute-start.35 = (f32[192,256]{1,0:T(8,128)}, f32[192,256]{1,0:T(8,128)S(1)}, u32[]{:S(2)}, u32[]{:S(2)}) collective-permute-start(f32[192,256]{1,0:T(8,128)} %get-tuple-element.143), channel_id=1, source_target_pairs={{0,16},{8,24},{16,0},{24,8},{1,17},{9,25},{17,1},{25,9},{2,18},{10... | collective-permute-start | bytes 589832 | tf_op jit(solution)/shard_map/ppermute | solution.py:175
  332.9 18.1 %collective-permute-start.36 = (f32[192,256]{1,0:T(8,128)}, f32[192,256]{1,0:T(8,128)S(1)}, u32[]{:S(2)}, u32[]{:S(2)}) collective-permute-start(f32[192,256]{1,0:T(8,128)} %get-tuple-element.144), channel_id=1, source_target_pairs={{0,24},{8,16},{16,8},{24,0},{1,25},{9,17},{17,9},{25,1},{2,26},{10... | collective-permute-start | bytes 589832 | tf_op jit(solution)/shard_map/ppermute | solution.py:175
  339.8 12.5 %collective-permute-start.24 = (f32[384,256]{1,0:T(8,128)}, f32[384,256]{1,0:T(8,128)S(1)}, u32[]{:S(2)}, u32[]{:S(2)}) collective-permute-start(f32[384,256]{1,0:T(8,128)} %get-tuple-element.120), channel_id=1, source_target_pairs={{0,24},{8,16},{16,8},{24,0},{1,25},{9,17},{17,9},{25,1},{2,26},{10... | collective-permute-start | bytes 1179656 | tf_op jit(solution)/shard_map/ppermute | solution.py:175
  (35 other events, 623.3 us)
